TPU v7x, 32 devices: a whole 2x2x4 slice. The times are simulated.
32 devices in a mesh: seg: 2 (over y), bank: 16 (over z, x, core).
Axes of the slice: x: 2, y: 2, z: 4, core: 2. Of those that a mesh axis runs over, the one named last changes fastest.
Arguments:
- strain: float32 [4, 2, 262144], P('seg', None, 'bank'), may hold values from -6 to 6
- templates: bfloat16 [64, 2, 262144], P('bank'), may hold values from -6 to 6
- counts: int32 [16], P('bank'), may hold values from 1 to 4, 24 in all
- edges: int32 [64, 17], P('bank'), may hold values from 1 to 262144, as said below
Outputs:
- slot_peak: float32 [64, 4], P('bank', 'seg')
- segment_peak: float32 [4], P('seg')
Inputs may be any that keep to these rules, and one draw needn't show every extreme that they name: counts[b] is the number of live slots of shard b, which are its first ones; some shard has all 4 slots live. Each row of edges rises strictly; its first and last edges lie more than 114688 bins apart, and each band holds about a 64th of that span or more.
All inputs are finite; a program needn't handle non-finite values.
Results may differ from a plain program's by a relative error of at most 0.0003.
Values may be sent and summed in bfloat16 or wider, within the bound.
No kernel may reach another device: no remote copies, remote signals or barrier semaphores. Data moves between devices by JAX's collectives and lax.ppermute only.
A program may use at most 128 MiB of HBM per device.

v0:
```python
import math

import jax
import jax.numpy as jnp
from jax import lax
from jax.sharding import PartitionSpec as P

CELL = 128
BINS = 16


EXACT = lax.Precision.HIGHEST
EPSILON = 1e-06


def phase_table(numbers, modulus):
    angle = numbers.astype(jnp.float32) * (2.0 * math.pi / modulus)
    return (jnp.cos(angle), jnp.sin(angle))


def ramp(count):
    return jnp.arange(count, dtype=jnp.int32)


def build_tables(spectrum_bins, cell):
    samples = 2 * spectrum_bins
    cells = samples // cell
    levels = cells.bit_length() - 1
    outer = 2 ** (levels // 2)
    centre = cells // outer
    first_lattice = phase_table(ramp(outer)[:, None] * ramp(outer)[None, :] % outer, outer)
    second_lattice = phase_table(ramp(centre)[:, None] * ramp(centre)[None, :] % centre, centre)
    grid_c = phase_table(ramp(cell // 2)[:, None] * ramp(cell)[None, :] % cell, cell)
    twist_one = phase_table(
        ramp(centre)[:, None, None] * ramp(cell)[None, None, :] % (centre * cell), centre * cell
    )
    spread_index = ramp(cell)[None, None, :] + cell * ramp(centre)[:, None, None]
    twist_two = phase_table(ramp(outer)[None, :, None] * spread_index % samples, samples)
    twist_coarse = phase_table(ramp(centre)[:, None] * ramp(outer)[None, :] % cells, cells)
    return (first_lattice, second_lattice, grid_c, twist_one, twist_two, twist_coarse)


def complex_multiply_apply(form, table, real, imaginary):
    cosine, sine = table
    out_real = jnp.einsum(form, cosine, real, precision=EXACT) - jnp.einsum(
        form, sine, imaginary, precision=EXACT
    )
    out_imag = jnp.einsum(form, cosine, imaginary, precision=EXACT) + jnp.einsum(
        form, sine, real, precision=EXACT
    )
    return (out_real, out_imag)


def twist(real, imaginary, table):
    cosine, sine = table
    return (real * cosine - imaginary * sine, real * sine + imaginary * cosine)


def fold_bands(stacked, edge_row, cells):
    rows = stacked.shape[1]
    lower = edge_row[:BINS]
    upper = edge_row[1:]
    low_row = lower // cells
    high_row = upper // cells
    row_index = ramp(rows)
    interior = (
        (row_index[None, :] > low_row[:, None]) & (row_index[None, :] < high_row[:, None])
    ).astype(jnp.float32)
    middle = jnp.einsum("bj,xjr->xbr", interior, stacked, precision=EXACT)
    column = ramp(cells)
    first_row = jnp.take(stacked, low_row, axis=1)
    first_bin = low_row[:, None] * cells + column[None, :]
    first_mask = (first_bin >= lower[:, None]) & (first_bin < upper[:, None])
    last_row = jnp.take(stacked, jnp.minimum(high_row, rows - 1), axis=1)
    last_bin = high_row[:, None] * cells + column[None, :]
    last_mask = (last_bin < upper[:, None]) & (high_row > low_row)[:, None]
    return (
        middle
        + jnp.where(first_mask[None], first_row, 0.0)
        + jnp.where(last_mask[None], last_row, 0.0)
    )


def slot_results(wave, edge_row, spectra, tables):
    first_lattice, second_lattice, grid_c, twist_one, twist_two, twist_coarse = tables
    centre, outer = twist_coarse[0].shape
    cell = grid_c[0].shape[1]
    cells = centre * outer
    spectrum_bins = wave.shape[1]
    rows = spectrum_bins // cells
    wave_real = wave[0].astype(jnp.float32)
    wave_imag = wave[1].astype(jnp.float32)
    index = ramp(spectrum_bins)
    inside = (index >= edge_row[0]) & (index < edge_row[BINS])
    power = jnp.where(inside, wave_real * wave_real + wave_imag * wave_imag, 0.0)
    band_power = jnp.sum(fold_bands(power.reshape(1, rows, cells), edge_row, cells)[0], axis=1)
    energy = jnp.sum(band_power)
    weight = band_power / energy
    results = []
    for segment in range(spectra.shape[0]):
        data_real = spectra[segment, 0]
        data_imag = spectra[segment, 1]
        product_real = jnp.where(inside, data_real * wave_real + data_imag * wave_imag, 0.0)
        product_imag = jnp.where(inside, data_imag * wave_real - data_real * wave_imag, 0.0)
        strain_section_real, strain_section_imaginary = complex_multiply_apply(
            "kt,kn->nt",
            grid_c,
            product_real.reshape(cell // 2, cells),
            product_imag.reshape(cell // 2, cells),
        )
        strain_section_real = strain_section_real.reshape(centre, outer, cell)
        strain_section_imaginary = strain_section_imaginary.reshape(centre, outer, cell)
        strain_section_real, strain_section_imaginary = twist(
            strain_section_real, strain_section_imaginary, twist_one
        )
        strain_section_real, strain_section_imaginary = complex_multiply_apply(
            "pm,mku->pku", second_lattice, strain_section_real, strain_section_imaginary
        )
        strain_section_real, strain_section_imaginary = twist(
            strain_section_real, strain_section_imaginary, twist_two
        )
        strain_section_real, strain_section_imaginary = complex_multiply_apply(
            "kt,bkc->btc", first_lattice, strain_section_real, strain_section_imaginary
        )
        loudness = jnp.sqrt(
            jnp.max(
                strain_section_real * strain_section_real
                + strain_section_imaginary * strain_section_imaginary,
                axis=2,
            )
        ) / jnp.sqrt(energy)
        folded = fold_bands(
            jnp.stack([product_real, product_imag]).reshape(2, rows, cells), edge_row, cells
        )
        frequency_band_real = folded[0].reshape(BINS, centre, outer)
        frequency_band_imaginary = folded[1].reshape(BINS, centre, outer)
        frequency_band_real, frequency_band_imaginary = complex_multiply_apply(
            "tq,bqp->btp", second_lattice, frequency_band_real, frequency_band_imaginary
        )
        frequency_band_real, frequency_band_imaginary = twist(
            frequency_band_real, frequency_band_imaginary, twist_coarse
        )
        frequency_band_real, frequency_band_imaginary = complex_multiply_apply(
            "sc,gns->gnc", first_lattice, frequency_band_real, frequency_band_imaginary
        )
        total_real = jnp.sum(frequency_band_real, axis=0)
        total_imag = jnp.sum(frequency_band_imaginary, axis=0)
        error_real = frequency_band_real - weight[:, None, None] * total_real[None]
        error_imag = frequency_band_imaginary - weight[:, None, None] * total_imag[None]
        misfit = jnp.sum(
            (error_real * error_real + error_imag * error_imag)
            / (band_power[:, None, None] + EPSILON),
            axis=0,
        )
        reduced = misfit / (2 * BINS - 2)
        factor = jnp.where(reduced > 1.0, ((1.0 + reduced**3) / 2.0) ** (-1.0 / 6.0), 1.0)
        results.append(jnp.max(loudness * factor))
    return jnp.stack(results)


def per_device(strain, templates, counts, edges):
    spectra = lax.all_gather(strain, "bank", axis=2, tiled=True)
    slots = templates.shape[0]
    segment_count = spectra.shape[0]
    tables = build_tables(templates.shape[2], CELL)

    def compute(results, position, source_waves, source_edges):
        wave = lax.dynamic_index_in_dim(source_waves, position, 0, keepdims=False)
        edge_row = lax.dynamic_index_in_dim(source_edges, position, 0, keepdims=False)
        values = slot_results(wave, edge_row, spectra, tables)
        return lax.dynamic_update_slice_in_dim(results, values[None], position, 0)

    def own_step(position, results):
        return compute(results, position, templates, edges)

    own_count = counts[0]
    slot_peak = lax.fori_loop(
        0, own_count, own_step, jnp.zeros((slots, segment_count), jnp.float32)
    )
    segment_peak = lax.pmax(jnp.max(slot_peak, axis=0), "bank")
    return (slot_peak, segment_peak)


def solution(mesh):
    placed = (P("seg", None, "bank"), P("bank", None, None), P("bank"), P("bank", None))
    return jax.shard_map(
        per_device,
        mesh=mesh,
        in_specs=placed,
        out_specs=(P("bank", "seg"), P("seg")),
        check_vma=False,
    )
```

profile of v0, /device:TPU:0, one launch (start us, length us, event | category | flops | bytes accessed | tf_op | source)
XLA Modules:
  0.0 1034.4 jit_solution(2028167128649869415)
XLA Ops:
  8.6 54.9 %all-gather.2.cloned.1.call-done = f32[2,2,262144]{2,1,0:T(2,128)} async-done(((f32[2,2,16384]{2,1,0:T(2,128)}), f32[2,2,262144]{2,1,0:T(2,128)}) %all-gather.2.cloned.1.call-update) | async-done | bytes 4194320 | tf_op jit(solution)/shard_map/all_gather | solution.py:162
  64.1 237.5 %while.17 = (s32[]{:T(128)}, f32[4,2]{1,0:T(4,128)}, s32[]{:T(128)}, s32[4,17]{1,0:T(4,128)}, f32[2,2,262144]{2,1,0:T(2,128)}, /*index=5*/bf16[4,2,262144]{2,1,0...) while((s32[]{:T(128)}, f32[4,2]{1,0:T(4,128)}, ...), condition=%wide.region_13.16_spmd.clone.clone.clone, body=%wide.region_0.15_spmd.clone.clone.clone.sunk | while | flops 10792833024 | bytes 272773824 | solution.py:177
  67.6 27.2 %fusion.615 = (f32[262144]{0:T(1024)}, f32[1,1,262144]{2,1,0:T(1,128)S(1)}, f32[262144]{0:T(1024)}, f32[1,1,262144]{2,1,0:T(1,128)}, f32[262144]{0:T(1024)}, /*i...) fusion(f32[]{:T(128)} %broadcast.1690, ...), kind=kLoop, calls=%fused_computation.484.clone.1 | loop fusion | flops 4456448 | bytes 15728652 | tf_op jit(solution)/shard_map/while/body/add | solution.py:95
  118.6 4.0 fusion.642
  135.1 3.5 gather_fusion.5
  138.6 3.5 gather_fusion.4
  162.1 3.5 gather_fusion
  177.7 4.8 fusion.621
  182.4 5.0 convolution_subtract_fusion.14
  187.4 4.7 fusion.620
  192.1 4.7 convolution_add_fusion.12
  196.8 5.3 fusion.623
  202.2 5.0 convolution_subtract_fusion.15
  207.1 5.1 fusion.622
  212.3 4.9 convolution_add_fusion.13
  217.3 4.8 fusion.618
  222.1 4.9 convolution_subtract_fusion.12
  227.1 4.7 fusion.617
  231.8 4.7 convolution_add_fusion.11
  236.5 5.4 fusion.624
  241.9 4.9 fusion.619
  246.9 4.9 convolution_subtract_fusion.13
  251.8 14.0 %fusion.625 = (f32[64,64,128]{2,0,1:T(8,128)S(1)}, f32[64,64,128]{2,0,1:T(8,128)S(1)}, f32[64,64,128]{2,0,1:T(8,128)S(1)}, f32[64,64,128]{2,0,1:T(8,128)S(1)}) fusion(f32[64,128,64]{1,2,0:T(8,128)S(1)} %convolution_subtract_fusion.13, s32[64,128]{1,0:T(8,128)S(1)} %copy-done.12, f32[64,128,64]{1,2,0:T(8,128)S(1)} %convolution_add_fusion.13, ...), kind=kOutput, calls=%fused_computation.45.clone.1 | convolution fusion | flops 418439168 | bytes 21069824 | tf_op jit(solution)/shard_map/while/body/pm,mku->pku/dot_general | solution.py:48
  265.8 3.4 fusion.628
  269.2 3.4 fusion.626
  272.6 3.4 fusion.627
  276.0 4.5 add_reduce_fusion.4
  281.2 3.4 fusion.657
  284.6 3.4 fusion.655
  288.0 3.6 fusion.656
  291.6 4.1 add_reduce_fusion.5
  303.6 723.6 %pmax.7 = f32[2]{0:T(128)} all-reduce(f32[2]{0:T(128)S(1)} %reduce_max.65), channel_id=1, replica_groups=mesh['seg'=2,'bank'=16] {'bank'}, use_global_device_ids=true, to_apply=%region_15.18 | all-reduce | flops 2 | bytes 16 | tf_op jit(solution)/shard_map/pmax | solution.py:180
  (109 shorter events, 78.0 us)
Async XLA Ops:
  7.2 56.3 %all-gather.2.cloned.1.call-start = ((), (), s32[]{:S(2)}) async-start(), calls=%async_computation | async-start | bytes 4456448 | tf_op jit(solution)/shard_map/all_gather | solution.py:162
  66.5 75.5 %copy-start.13 = (pred[16]{0:T(512)(128)(4,1)}, pred[16]{0:T(512)(128)(4,1)S(1)}, u32[]{:S(2)}) copy-start(pred[16]{0:T(512)(128)(4,1)S(1)} %get-tuple-element.823) | copy-start | bytes 52 | tf_op jit(solution)/shard_map/while
  66.5 75.5 %copy-start.15 = (pred[16]{0:T(512)(128)(4,1)}, pred[16]{0:T(512)(128)(4,1)S(1)}, u32[]{:S(2)}) copy-start(pred[16]{0:T(512)(128)(4,1)S(1)} %get-tuple-element.822) | copy-start | bytes 52 | tf_op jit(solution)/shard_map/while
  67.0 75.0 %copy-start.8 = (pred[16,4096]{1,0:T(8,128)(4,1)}, pred[16,4096]{1,0:T(8,128)(4,1)S(1)}, u32[]{:S(2)}) copy-start(pred[16,4096]{1,0:T(8,128)(4,1)S(1)} %get-tuple-element.829) | copy-start | bytes 196612 | tf_op jit(solution)/shard_map/while
  67.1 75.0 %copy-start.10 = (pred[16,4096]{1,0:T(8,128)(4,1)}, pred[16,4096]{1,0:T(8,128)(4,1)S(1)}, u32[]{:S(2)}) copy-start(pred[16,4096]{1,0:T(8,128)(4,1)S(1)} %get-tuple-element.828) | copy-start | bytes 196612 | tf_op jit(solution)/shard_map/while
  118.6 8.3 copy-start.5
  131.0 1.0 copy-start
  159.4 6.2 copy-start.9
  159.4 6.2 copy-start.11
  159.4 6.2 copy-start.14
  159.4 6.2 copy-start.16
  175.0 2.2 copy-start.6
  175.0 2.2 copy-start.7
  175.0 2.2 copy-start.17
  175.0 2.2 copy-start.18
  176.1 1.6 copy-start.4
  177.6 4.8 copy-start.2
  212.3 5.0 copy-start.3
  217.3 4.8 copy-start.1
  246.8 5.0 copy-start.12
Sparse Core Ops, SparseCore 0:
  10.2 53.2 all-gather.1
where the time goes:
time: 1040 us; the launch traced here: 1030 us
  blocking collectives  724 us (70%)
  matrix products  146 us (14%)
  waiting for transfers between devices  55.6 us (5%)
  local copies, waits for them, and re-layouts  47.9 us (5%)
  other arithmetic  42.3 us (4%)
  between operations  14.3 us (1%)
    pmax x1, blocking collectives, per_device(): segment_peak = lax.pmax(jnp.max(slot_peak, axis=0), 'bank')  724 us
    all_gather x1, waiting for transfers between devices, per_device(): spectra = lax.all_gather(strain, 'bank', axis=2, tiled=True)  54.9 us
    dot_general x10, matrix products, complex_multiply_apply(): jnp.einsum(form, sine, real, precision=EXACT)  41.1 us
    dot_general x10, matrix products, complex_multiply_apply(): jnp.einsum(form, cosine, real, precision=EXACT)  32.6 us
    dot_general x10, matrix products, complex_multiply_apply(): jnp.einsum(form, sine, imaginary, precision=EXACT)  31.8 us
    dot_general x10, matrix products, complex_multiply_apply(): jnp.einsum(form, cosine, imaginary, precision=EXACT)  30.9 us
    add x1, other arithmetic, slot_results(): wave_real * wave_real + wave_imag * wave_imag  27.2 us
  transfers between devices with their start and end apart: 1, of which 1 were waited for; matrix products, arithmetic and copies ran while one was open for 0% of the time, Pallas kernels for 0%

commit v1 on v0

v1 whole, which is shorter than its diff:
```python
import numpy as np

import jax
import jax.numpy as jnp
from jax import lax
from jax.experimental import pallas as pl
from jax.experimental.pallas import tpu as pltpu
from jax.sharding import PartitionSpec as P

CELL = 128
BINS = 16
EPSILON = 1e-06
ROWS = 512
HALF = 256
QUART = 128
CHUNK = 32


def split_bf16(x):
    high = x.astype(jnp.bfloat16)
    low = (x - high.astype(jnp.float32)).astype(jnp.bfloat16)
    return high, low


def host_split(x):
    high = x.astype(np.float32).astype(jnp.bfloat16)
    low = (x - high.astype(np.float64)).astype(np.float32).astype(jnp.bfloat16)
    return high, low


def host_tables():
    k = np.arange(HALF)
    u = np.arange(QUART) + 0.5
    angle = 2 * np.pi * u[:, None] * k[None, :] / HALF
    wave = np.concatenate([np.cos(angle), np.sin(angle)], axis=0)
    high, low = host_split(wave)
    first = np.concatenate([high, high, low], axis=1)
    second = np.concatenate([high.T, high.T, low.T], axis=0)
    eight = 2 * np.pi * (np.arange(8)[:, None] * np.arange(8)[None, :] % 8) / 8
    block = np.block([[np.cos(eight), -np.sin(eight)], [np.sin(eight), np.cos(eight)]])
    high, low = host_split(block)
    octet = np.concatenate([high, high, low], axis=1)
    angle = 2 * np.pi * k[None, :] * np.array([-2, -1, 1])[:, None] / 1024
    rows = np.stack([np.cos(angle), np.sin(angle)], axis=1)
    rows = np.broadcast_to(rows[..., None], rows.shape + (128,)).astype(np.float32)
    t0 = np.stack([np.stack([4 * np.arange(QUART) + v, 4 * (255 - np.arange(QUART)) + v]) for v in range(4)])
    angle = 2 * np.pi * ((t0[..., None] * np.arange(ROWS)) % (1 << 19)) / (1 << 19)
    between = np.stack([np.cos(angle), np.sin(angle)], axis=2).astype(np.float32)
    angle = 2 * np.pi * (128 * np.arange(8)[:, None] * np.arange(ROWS)[None, :]) / (1 << 19)
    coarse = np.stack([np.cos(angle), np.sin(angle)]).astype(np.float32)
    angle = -2 * np.pi * k / ROWS
    lanes = np.stack([np.cos(angle), np.sin(angle)]).astype(np.float32)
    lanes = np.broadcast_to(lanes[:, None, :], (2, 8, HALF)).copy()
    return first, second, octet, rows.copy(), between, coarse, lanes


def lane_butterfly(real, imag, lanes_real, lanes_imag):
    low_r, high_r = real[:, :HALF], real[:, HALF:]
    low_i, high_i = imag[:, :HALF], imag[:, HALF:]
    sum_r, sum_i = low_r + high_r, low_i + high_i
    even_r = sum_r * lanes_real - sum_i * lanes_imag
    even_i = sum_r * lanes_imag + sum_i * lanes_real
    return even_r, even_i, low_r - high_r, low_i - high_i


def split_dot(high, low, second_ref):
    return jnp.dot(
        jnp.concatenate([high, low, high], axis=1), second_ref[...], preferred_element_type=jnp.float32
    )


def make_kernel(slots):
    def kernel(
        plan_ref, edge_ref, strain_ref, wave_ref, first_ref, second_ref, octet_ref, rows_ref, between_ref,
        coarse_ref, lanes_ref, out_ref, q_ref, p_ref, x_ref, o_ref, l_ref, z_ref, fold_ref, peak_ref,
    ):
        step = pl.program_id(0)

        @pl.when(step == 0)
        def _():
            out_ref[...] = jnp.zeros_like(out_ref)

        @pl.when(step < plan_ref[slots])
        def _():
            slot = plan_ref[step]
            core = plan_ref[slots + 1]
            base = slot * (BINS + 1)
            first_edge = edge_ref[base]
            last_edge = edge_ref[base + BINS]

            held = strain_ref.shape[3]
            piece = min(held, 16)

            def strain_rows(part, r):
                pieces = []
                for i in range(16 // piece):
                    row = r + i * piece
                    owner = row // held
                    which = (owner + core) % 2
                    inner = pl.multiple_of(row % held, piece)
                    pieces.append(strain_ref[owner // 2, which, part, pl.ds(inner, piece), :])
                return pieces[0] if len(pieces) == 1 else jnp.concatenate(pieces, axis=0)

            def product(r):
                data_r = strain_rows(0, r)
                data_i = strain_rows(1, r)
                wave_r = wave_ref[0, 0, pl.ds(r, 16), :].astype(jnp.float32)
                wave_i = wave_ref[0, 1, pl.ds(r, 16), :].astype(jnp.float32)
                index = (
                    lax.broadcasted_iota(jnp.int32, (16, ROWS), 0) * ROWS
                    + lax.broadcasted_iota(jnp.int32, (16, ROWS), 1)
                    + r * ROWS
                )
                inside = (index >= first_edge) & (index < last_edge)
                real = jnp.where(inside, data_r * wave_r + data_i * wave_i, 0.0)
                imag = jnp.where(inside, data_i * wave_r - data_r * wave_i, 0.0)
                q_ref[0, pl.ds(r, 16), :] = real
                q_ref[1, pl.ds(r, 16), :] = imag
                p_ref[pl.ds(r, 16), :] = wave_r * wave_r + wave_i * wave_i
                return real, imag

            def front(c, carry):
                r = pl.multiple_of(c * 16, 16)
                low_r, low_i = product(r)
                high_r, high_i = product(pl.multiple_of(r + HALF, 16))
                mixed = [
                    (low_r + high_r, low_i + high_i),
                    (low_r - high_i, low_i + high_r),
                    (low_r - high_r, low_i - high_i),
                    (low_r + high_i, low_i - high_r),
                ]
                for v in range(4):
                    real, imag = mixed[v]
                    if v != 2:
                        at = (0, 1, 0, 2)[v]
                        cosine = jnp.concatenate([rows_ref[at, 0, pl.ds(r, 16), :]] * 4, axis=1)
                        sine = jnp.concatenate([rows_ref[at, 1, pl.ds(r, 16), :]] * 4, axis=1)
                        real, imag = real * cosine - imag * sine, real * sine + imag * cosine
                    for part, value in ((0, real), (1, imag)):
                        high, low = split_bf16(value)
                        column = (2 * v + part) * ROWS
                        x_ref[pl.ds(r, 16), column : column + ROWS] = high
                        x_ref[pl.ds(pl.multiple_of(r + HALF, 16), 16), column : column + ROWS] = low
                return carry

            lax.fori_loop(0, HALF // 16, front, 0)

            offset = lax.broadcasted_iota(jnp.int32, (8, ROWS), 0) * ROWS + lax.broadcasted_iota(
                jnp.int32, (8, ROWS), 1
            )
            powers = []
            for b in range(BINS):
                lower = edge_ref[base + b]
                upper = edge_ref[base + b + 1]

                def gather(i, carry, lower=lower, upper=upper):
                    real, imag, power = carry
                    r = pl.multiple_of(i * 8, 8)
                    start = i * (8 * ROWS)
                    mask = (offset >= lower - start) & (offset < upper - start)
                    real = real + jnp.where(mask, q_ref[0, pl.ds(r, 8), :], 0.0)
                    imag = imag + jnp.where(mask, q_ref[1, pl.ds(r, 8), :], 0.0)
                    power = power + jnp.where(mask, p_ref[pl.ds(r, 8), :], 0.0)
                    return real, imag, power

                zero = jnp.zeros((8, ROWS), jnp.float32)
                real, imag, power = lax.fori_loop(
                    lower // (8 * ROWS), (upper + (8 * ROWS - 1)) // (8 * ROWS), gather, (zero, zero, zero)
                )
                fold_ref[0:8, b * ROWS : (b + 1) * ROWS] = real
                fold_ref[8:16, b * ROWS : (b + 1) * ROWS] = imag
                powers.append(jnp.sum(power, axis=(0, 1), keepdims=True))
            energy = powers[0]
            for b in range(1, BINS):
                energy = energy + powers[b]

            lanes_r = lanes_ref[0, 0:1, :]
            lanes_i = lanes_ref[1, 0:1, :]

            for v in range(4):
                column = v * 2 * ROWS
                whole = jnp.dot(
                    first_ref[...],
                    jnp.concatenate(
                        [x_ref[:, column : column + 2 * ROWS], x_ref[0:HALF, column : column + 2 * ROWS]], axis=0
                    ),
                    preferred_element_type=jnp.float32,
                )
                o_ref[...] = whole
                for chunk in range(QUART // CHUNK):
                    u = chunk * CHUNK
                    cos_r = o_ref[u : u + CHUNK, :ROWS]
                    cos_i = o_ref[u : u + CHUNK, ROWS:]
                    sin_r = o_ref[QUART + u : QUART + u + CHUNK, :ROWS]
                    sin_i = o_ref[QUART + u : QUART + u + CHUNK, ROWS:]
                    for mirror in range(2):
                        if mirror == 0:
                            real, imag = cos_r - sin_i, cos_i + sin_r
                        else:
                            real, imag = cos_r + sin_i, cos_i - sin_r
                        cosine = between_ref[v, mirror, 0, u : u + CHUNK, :]
                        sine = between_ref[v, mirror, 1, u : u + CHUNK, :]
                        real, imag = real * cosine - imag * sine, real * sine + imag * cosine
                        values = lane_butterfly(real, imag, lanes_r, lanes_i)
                        for part in range(4):
                            high, low = split_bf16(values[part])
                            at = ((chunk * 2 + mirror) * 4 + part) * CHUNK
                            l_ref[at : at + CHUNK, :HALF] = high
                            l_ref[at : at + CHUNK, HALF:] = low
                z_ref[...] = jnp.dot(
                    jnp.concatenate([l_ref[...], l_ref[:, :HALF]], axis=1),
                    second_ref[...],
                    preferred_element_type=jnp.float32,
                )
                for chunk in range(QUART // CHUNK):
                    for mirror in range(2):
                        cell = chunk if mirror == 0 else 7 - chunk
                        for parity in range(2):
                            at = ((chunk * 2 + mirror) * 4 + parity * 2) * CHUNK
                            real = z_ref[at : at + CHUNK, :]
                            imag = z_ref[at + CHUNK : at + 2 * CHUNK, :]
                            a, d = real[:, :128], real[:, 128:]
                            c, e = imag[:, :128], imag[:, 128:]
                            for side in range(2):
                                if side == 0:
                                    re, im = a - e, c + d
                                else:
                                    re, im = a + e, c - d
                                square = re * re + im * im
                                best = jnp.max(square.reshape(CHUNK // 8, 8, 128), axis=0)
                                lane = (parity * 2 + side) * 128
                                if v:
                                    best = jnp.maximum(best, peak_ref[cell, :, lane : lane + 128])
                                peak_ref[cell, :, lane : lane + 128] = best

            high, low = split_bf16(fold_ref[...])
            bands = jnp.dot(
                octet_ref[...], jnp.concatenate([high, low, high], axis=0), preferred_element_type=jnp.float32
            )
            parts = [[], [], [], []]
            coarse_r = coarse_ref[0]
            coarse_i = coarse_ref[1]
            for b in range(BINS):
                real = bands[0:8, b * ROWS : (b + 1) * ROWS]
                imag = bands[8:16, b * ROWS : (b + 1) * ROWS]
                real, imag = real * coarse_r - imag * coarse_i, real * coarse_i + imag * coarse_r
                values = lane_butterfly(real, imag, lanes_r, lanes_i)
                for part in range(4):
                    parts[part].append(values[part])
            left = jnp.concatenate([value for part in parts for value in part], axis=0)
            high, low = split_bf16(left)
            result = split_dot(high, low, second_ref)
            loud = jnp.concatenate(
                [jnp.max(peak_ref[cell], axis=0, keepdims=True) for cell in range(8)], axis=0
            )
            inverse = 1.0 / energy
            top = jnp.zeros((8, 128), jnp.float32)
            for parity in range(2):
                real = result[parity * 256 : parity * 256 + 128, :]
                imag = result[parity * 256 + 128 : parity * 256 + 256, :]
                a, d = real[:, :128], real[:, 128:]
                c, e = imag[:, :128], imag[:, 128:]
                for side in range(2):
                    if side == 0:
                        re, im = a - e, c + d
                    else:
                        re, im = a + e, c - d
                    re = re.reshape(BINS, 8, 128)
                    im = im.reshape(BINS, 8, 128)
                    total_r = jnp.sum(re, axis=0)
                    total_i = jnp.sum(im, axis=0)
                    misfit = jnp.zeros((8, 128), jnp.float32)
                    for b in range(BINS):
                        weight = powers[b] * inverse
                        error_r = re[b] - weight * total_r
                        error_i = im[b] - weight * total_i
                        misfit = misfit + (error_r * error_r + error_i * error_i) * (1.0 / (powers[b] + EPSILON))
                    reduced = misfit / (2 * BINS - 2)
                    factor = jnp.where(
                        reduced > 1.0, jnp.exp(jnp.log((1.0 + reduced * reduced * reduced) / 2.0) * (-1.0 / 6.0)), 1.0
                    )
                    lane = (parity * 2 + side) * 128
                    top = jnp.maximum(top, jnp.sqrt(loud[:, lane : lane + 128]) * factor)
            best = jnp.max(top, axis=(0, 1), keepdims=True) / jnp.sqrt(energy)
            out_ref[pl.ds(slot, 1), :] = jnp.broadcast_to(best, (1, 128))

    return kernel


def slot_peaks(plan, edges, strain, waves, interpret=False):
    slots = waves.shape[0]
    tables = [jnp.asarray(table) for table in host_tables()]

    def resident(array):
        return pl.BlockSpec(
            array.shape, lambda i, plan, edges, n=array.ndim: (0,) * n, pipeline_mode=pl.Buffered(1)
        )

    return pl.pallas_call(
        make_kernel(slots),
        out_shape=jax.ShapeDtypeStruct((slots, 128), jnp.float32),
        grid_spec=pltpu.PrefetchScalarGridSpec(
            num_scalar_prefetch=2,
            grid=(slots,),
            in_specs=[
                resident(strain),
                pl.BlockSpec((1, 2, ROWS, ROWS), lambda i, plan, edges: (plan[i], 0, 0, 0)),
            ]
            + [resident(table) for table in tables],
            out_specs=pl.BlockSpec((slots, 128), lambda i, plan, edges: (0, 0)),
            scratch_shapes=[
                pltpu.VMEM((2, ROWS, ROWS), jnp.float32),
                pltpu.VMEM((ROWS, ROWS), jnp.float32),
                pltpu.VMEM((ROWS, 8 * ROWS), jnp.bfloat16),
                pltpu.VMEM((HALF, 2 * ROWS), jnp.float32),
                pltpu.VMEM((1024, ROWS), jnp.bfloat16),
                pltpu.VMEM((1024, HALF), jnp.float32),
                pltpu.VMEM((16, BINS * ROWS), jnp.float32),
                pltpu.VMEM((8, 8, ROWS), jnp.float32),
            ],
        ),
        compiler_params=pltpu.CompilerParams(vmem_limit_bytes=48 << 20),
        interpret=interpret,
    )(plan, edges, strain, waves, *tables)


def per_device(strain, templates, counts, edges):
    devices = lax.axis_size("bank")
    device = lax.axis_index("bank")
    core = device % 2
    slots = templates.shape[0]
    mates = [(i, i ^ 1) for i in range(devices)]
    cores = [list(range(c, devices, 2)) for c in range(2)]

    shard = strain.reshape(2, 2, -1, ROWS)
    own = lax.dynamic_index_in_dim(shard, core, 0, keepdims=False)
    other = lax.dynamic_index_in_dim(shard, 1 - core, 0, keepdims=False)
    shard = jnp.stack([own, lax.ppermute(other, "bank", mates)])
    spectrum = lax.all_gather(shard, "bank", axis=0, tiled=False, axis_index_groups=cores)

    small = jnp.concatenate([counts, edges.reshape(-1)])
    mate_small = lax.ppermute(small, "bank", mates)
    mate_waves = lax.ppermute(templates, "bank", mates)
    waves = jnp.concatenate([templates, mate_waves]).reshape(2 * slots, 2, ROWS, ROWS)
    own_count = small[0]
    live = own_count + mate_small[0]
    ramp = jnp.minimum(jnp.arange(2 * slots, dtype=jnp.int32), live - 1)
    order = jnp.where(ramp < own_count, ramp, slots + ramp - own_count)
    plan = jnp.concatenate([order, live[None], core[None]]).astype(jnp.int32)
    all_edges = jnp.concatenate([small[1:], mate_small[1:]])
    peaks = slot_peaks(plan, all_edges, spectrum, waves)[:, 0]

    mine = peaks[:slots]
    theirs = lax.ppermute(peaks[slots:], "bank", mates)
    slot_peak = jnp.where(core == 0, jnp.stack([mine, theirs], axis=1), jnp.stack([theirs, mine], axis=1))
    segment_peak = lax.pmax(jnp.max(slot_peak, axis=0), "bank")
    return (slot_peak, segment_peak)


def solution(mesh):
    placed = (P("seg", None, "bank"), P("bank", None, None), P("bank"), P("bank", None))
    return jax.shard_map(
        per_device,
        mesh=mesh,
        in_specs=placed,
        out_specs=(P("bank", "seg"), P("seg")),
        check_vma=False,
    )
```

time: 1040 us -> 160 us (0.15)
  blocking collectives: 724 us -> 30.2 us
  matrix products: 146 us -> 0 us
  Pallas kernels: 0 us -> 50.8 us
  local copies, waits for them, and re-layouts: 47.9 us -> 16.8 us
  other arithmetic: 42.3 us -> 14.3 us
  waiting for transfers between devices: 55.6 us -> 31.1 us
    pmax x1, blocking collectives: 724 us -> 30.2 us  [per_device(): segment_peak = lax.pmax(jnp.max(slot_peak, axis=0), 'bank')]
    dot_general x43 -> x0, matrix products: 146 us -> none  [the longest x10 41.1 us: complex_multiply_apply(): jnp.einsum(form, sine, real, precision=EXACT)]
    pallas_call x0 -> x1, Pallas kernels: none -> 50.8 us  [slot_peaks(): pl.pallas_call(make_kernel(slots), out_shape=jax.ShapeDtypeStruct((slots,...]
    all_gather x1, waiting for transfers between devices: 54.9 us -> 26.4 us  [per_device(): lax.all_gather(shard, 'bank', axis=0, tiled=False, axis_index_groups=cores)]
    add x2 -> x0, other arithmetic: 27.8 us -> none  [the longest x1 27.2 us: slot_results(): wave_real * wave_real + wave_imag * wave_imag]
    gather x6 -> x0, local copies, waits for them, and re-layouts: 15.8 us -> none  [the longest x3 8.24 us: fold_bands(): last_row = jnp.take(stacked, jnp.minimum(high_row, rows - 1), axis=1)]
    reshape x0 -> x3, local copies, waits for them, and re-layouts: none -> 14.2 us  [the longest x1 12.3 us: per_device(): jnp.concatenate([templates, mate_waves]).reshape(2 * slots, 2, ROWS, ROWS)]
    concatenate x0 -> x4, other arithmetic: none -> 13.4 us  [the longest x1 13.2 us: per_device(): jnp.concatenate([templates, mate_waves]).reshape(2 * slots, 2, ROWS, ROWS)]
  transfers between devices with their start and end apart: 1 -> 5, of which waited for: 1 -> 3; matrix products, arithmetic and copies ran while one was open for 0% -> 18% of each run, Pallas kernels for 0% -> 0%
where the time goes in v1:
time: 160 us; the launch traced here: 159 us
  Pallas kernels  50.8 us (32%)
  waiting for transfers between devices  31.1 us (19%)
  blocking collectives  30.2 us (19%)
  local copies, waits for them, and re-layouts  16.8 us (10%)
  between operations  14.9 us (9%)
  other arithmetic  14.3 us (9%)
    pallas_call x1, Pallas kernels, slot_peaks(): pl.pallas_call(make_kernel(slots), out_shape=jax.ShapeDtypeStruct((slots,...  50.8 us
    pmax x1, blocking collectives, per_device(): segment_peak = lax.pmax(jnp.max(slot_peak, axis=0), 'bank')  30.2 us
    all_gather x1, waiting for transfers between devices, per_device(): lax.all_gather(shard, 'bank', axis=0, tiled=False, axis_index_groups=cores)  26.4 us
    concatenate x1, other arithmetic, per_device(): jnp.concatenate([templates, mate_waves]).reshape(2 * slots, 2, ROWS, ROWS)  13.2 us
    reshape x1, local copies, waits for them, and re-layouts, per_device(): jnp.concatenate([templates, mate_waves]).reshape(2 * slots, 2, ROWS, ROWS)  12.3 us
    ppermute x1, waiting for transfers between devices, per_device(): mate_small = lax.ppermute(small, 'bank', mates)  3.49 us
  transfers between devices with their start and end apart: 5, of which 3 were waited for; matrix products, arithmetic and copies ran while one was open for 18% of the time, Pallas kernels for 0%

profile of v1, /device:TPU:0, one launch (start us, length us, event | category | flops | bytes accessed | tf_op | source)
XLA Modules:
  0.0 159.1 jit_solution(12708821698241988310)
XLA Ops:
  7.2 0.0 all-gather.3.cloned.1.call-start
  7.2 0.5 collective-permute-start.2
  8.4 0.8 reshape.16
  9.1 0.1 pad_add_fusion.1
  9.2 0.1 collective-permute-start
  9.3 1.2 reshape.17
  10.5 0.5 collective-permute-start.1
  11.0 3.5 %collective-permute-done = s32[69]{0:T(128)S(1)} collective-permute-done((s32[69]{0:T(128)S(1)}, s32[69]{0:T(128)S(1)}, u32[]{:S(2)}, u32[]{:S(2)}) %collective-permute-start) | collective-permute-done | bytes 308 | tf_op jit(solution)/shard_map/ppermute | solution.py:342
  14.6 0.1 pad_add_fusion.2.plan_ref
  14.6 0.1 slice.20
  14.7 0.1 pad_add_fusion.edge_ref
  14.8 0.0 collective-permute-done.1
  14.8 0.7 pad_maximum_fusion.1
  15.5 0.0 all-gather.3.cloned.1.call-update
  15.6 13.2 %pad_maximum_fusion = bf16[8,2,262144]{2,1,0:T(2,128)(2,1)} fusion(bf16[4,2,262144]{2,1,0:T(2,128)(2,1)} %collective-permute-done.2, bf16[4,2,262144]{2,1,0:T(2,128)(2,1)} %param.12), kind=kLoop, calls=%fused_computation | loop fusion | flops 4194304 | bytes 16777216 | tf_op jit(solution)/shard_map/concatenate | solution.py:344
  28.8 0.0 copy-start.1
  28.8 0.0 copy-start.2
  28.8 0.0 copy-start.3
  28.8 0.0 copy-start.4
  28.8 0.0 copy-start.5
  28.8 0.0 copy-start.6
  28.8 12.3 %reshape.18.wave_ref = bf16[8,2,512,512]{3,2,1,0:T(8,128)(2,1)} reshape(bf16[8,2,262144]{2,1,0:T(2,128)(2,1)} %pad_maximum_fusion) | data formatting | bytes 16777216 | tf_op jit(solution)/shard_map/reshape | solution.py:344
  41.1 26.4 %all-gather.3.cloned.1.call-done = f32[16,2,32,512]{3,2,1,0:T(8,128)} async-done(((f32[2,2,32,512]{3,2,1,0:T(8,128)}), f32[16,2,32,512]{3,2,1,0:T(8,128)}) %all-gather.3.cloned.1.call-update) | async-done | bytes 2097168 | tf_op jit(solution)/shard_map/all_gather | solution.py:339
  67.6 1.6 copy-done
  69.2 50.8 %shard_map.122 = f32[8,128]{1,0:T(8,128)S(1)} custom-call(s32[10]{0:T(128)S(1)} %pad_add_fusion.2.plan_ref, s32[136]{0:T(256)S(1)} %pad_add_fusion.edge_ref, f32[8,2,2,32,512]{4,3,2,1,0:T(8,128)S(1)} %bitcast.12, bf16[8,2,512,512]{3,2,1,0:T(8,128)(2,1)} %reshape.18.wave_ref, bf16[256,768]{1,0:T(8,128)(2,1)S(1)} %copy-done.3, bf16[768,256]{1,0:T(8,128)(2,1)S(1)} %copy-done.2, ...), custom_call_target="tpu_custom_call" | custom-call | tf_op jit(solution)/shard_map/pallas_call | solution.py:299
  120.0 0.1 slice_reduce_fusion
  120.1 0.1 collective-permute-start.3
  120.2 1.1 collective-permute-done.3
  121.3 0.1 copy.19
  121.4 0.1 fusion
  121.5 30.2 %pmax.7 = f32[2]{0:T(128)} all-reduce(f32[2]{0:T(128)S(1)} %get-tuple-element.8), channel_id=1, replica_groups=mesh['seg'=2,'bank'=16] {'bank'}, use_global_device_ids=true, to_apply=%region_1.2 | all-reduce | flops 2 | bytes 16 | tf_op jit(solution)/shard_map/pmax | solution.py:356
  151.6 0.6 copy.21
  (10 shorter events, 0.0 us)
Async XLA Ops:
  7.2 60.4 %all-gather.3.cloned.1.call-start = ((), (), s32[]{:S(2)}) async-start(), calls=%async_computation | async-start | bytes 2359296 | tf_op jit(solution)/shard_map/all_gather | solution.py:339
  7.2 8.3 %collective-permute-start.2 = (bf16[4,2,262144]{2,1,0:T(2,128)(2,1)}, bf16[4,2,262144]{2,1,0:T(2,128)(2,1)}, u32[]{:S(2)}, u32[]{:S(2)}) collective-permute-start(bf16[4,2,262144]{2,1,0:T(2,128)(2,1)} %param.12), channel_id=1, source_target_pairs={{0,1},{1,0},{2,3},{3,2},{4,5},{5,4},{6,7},{7,6},{8,9},{9,8},{10,11... | collective-permute-start | bytes 12582920 | tf_op jit(solution)/shard_map/ppermute | solution.py:343
  9.2 5.3 %collective-permute-start = (s32[69]{0:T(128)S(1)}, s32[69]{0:T(128)S(1)}, u32[]{:S(2)}, u32[]{:S(2)}) collective-permute-start(s32[69]{0:T(128)S(1)} %pad_add_fusion.1), channel_id=1, source_target_pairs={{0,1},{1,0},{2,3},{3,2},{4,5},{5,4},{6,7},{7,6},{8,9},{9,8},{10,11... | collective-permute-start | bytes 836 | tf_op jit(solution)/shard_map/ppermute | solution.py:342
  10.5 4.3 %collective-permute-start.1 = (f32[2,32,512]{2,1,0:T(8,128)S(1)}, f32[2,32,512]{2,1,0:T(8,128)S(1)}, u32[]{:S(2)}, u32[]{:S(2)}) collective-permute-start(f32[2,32,512]{2,1,0:T(8,128)S(1)} %get-tuple-element.11), channel_id=1, source_target_pairs={{0,1},{1,0},{2,3},{3,2},{4,5},{5,4},{6,7},{7,6},{8,9},{9,8},{10,11... | collective-permute-start | bytes 393224 | tf_op jit(solution)/shard_map/ppermute | solution.py:338
  28.8 38.8 %copy-start.1 = (f32[3,2,256,128]{3,2,1,0:T(8,128)S(1)}, f32[3,2,256,128]{3,2,1,0:T(8,128)}, u32[]{:S(2)}) copy-start(f32[3,2,256,128]{3,2,1,0:T(8,128)} %constant.50.clone.rows_ref) | copy-start | bytes 2359300
  28.8 38.8 %copy-start.2 = (bf16[768,256]{1,0:T(8,128)(2,1)S(1)}, bf16[768,256]{1,0:T(8,128)(2,1)}, u32[]{:S(2)}) copy-start(bf16[768,256]{1,0:T(8,128)(2,1)} %constant.48.clone.second_ref) | copy-start | bytes 1179652
  28.8 38.8 %copy-start.3 = (bf16[256,768]{1,0:T(8,128)(2,1)S(1)}, bf16[256,768]{1,0:T(8,128)(2,1)}, u32[]{:S(2)}) copy-start(bf16[256,768]{1,0:T(8,128)(2,1)} %constant.47.clone.first_ref) | copy-start | bytes 1179652
  28.8 38.8 %copy-start.4 = (f32[2,8,512]{2,1,0:T(8,128)S(1)}, f32[2,8,512]{2,1,0:T(8,128)}, u32[]{:S(2)}) copy-start(f32[2,8,512]{2,1,0:T(8,128)} %constant.52.clone.coarse_ref) | copy-start | bytes 98308
  28.8 38.8 %copy-start.5 = (f32[2,8,256]{2,1,0:T(8,128)S(1)}, f32[2,8,256]{2,1,0:T(8,128)}, u32[]{:S(2)}) copy-start(f32[2,8,256]{2,1,0:T(8,128)} %constant.53.clone.lanes_ref) | copy-start | bytes 49156
  28.8 38.8 %copy-start.6 = (bf16[16,48]{1,0:T(8,128)(2,1)S(1)}, bf16[16,48]{1,0:T(8,128)(2,1)}, u32[]{:S(2)}) copy-start(bf16[16,48]{1,0:T(8,128)(2,1)} %constant.49.clone.octet_ref) | copy-start | bytes 4612
  67.6 1.6 %copy-start = (f32[16,2,32,512]{3,2,1,0:T(8,128)S(1)}, f32[16,2,32,512]{3,2,1,0:T(8,128)}, u32[]{:S(2)}) copy-start(f32[16,2,32,512]{3,2,1,0:T(8,128)} %all-gather.3.cloned.1.call-done) | copy-start | bytes 6291460
  120.1 1.2 collective-permute-start.3
Sparse Core Ops, SparseCore 0:
  15.7 51.8 all-gather.2

commit v2 on v1

--- a/solution.py
+++ b/solution.py
@@ -40,18 +40,20 @@
     block = np.block([[np.cos(eight), -np.sin(eight)], [np.sin(eight), np.cos(eight)]])
     high, low = host_split(block)
     octet = np.concatenate([high, high, low], axis=1)
-    angle = 2 * np.pi * k[None, :] * np.array([-2, -1, 1])[:, None] / 1024
+    angle = 2 * np.pi * k[None, :] * np.array([1, 2])[:, None] / 1024
     rows = np.stack([np.cos(angle), np.sin(angle)], axis=1)
     rows = np.broadcast_to(rows[..., None], rows.shape + (128,)).astype(np.float32)
-    t0 = np.stack([np.stack([4 * np.arange(QUART) + v, 4 * (255 - np.arange(QUART)) + v]) for v in range(4)])
-    angle = 2 * np.pi * ((t0[..., None] * np.arange(ROWS)) % (1 << 19)) / (1 << 19)
-    between = np.stack([np.cos(angle), np.sin(angle)], axis=2).astype(np.float32)
-    angle = 2 * np.pi * (128 * np.arange(8)[:, None] * np.arange(ROWS)[None, :]) / (1 << 19)
+    unit = 2 * np.pi / (1 << 19)
+    angle = unit * (4 * np.arange(QUART)[:, None] * np.arange(ROWS))
+    between = np.stack([np.cos(angle), np.sin(angle)]).astype(np.float32)
+    angle = unit * (np.array([0, 1, 2, 3, 1020, 1021, 1022, 1023])[:, None] * np.arange(ROWS))
+    shift = np.stack([np.cos(angle), np.sin(angle)]).astype(np.float32)
+    angle = unit * (128 * np.arange(8)[:, None] * np.arange(ROWS)[None, :])
     coarse = np.stack([np.cos(angle), np.sin(angle)]).astype(np.float32)
     angle = -2 * np.pi * k / ROWS
     lanes = np.stack([np.cos(angle), np.sin(angle)]).astype(np.float32)
     lanes = np.broadcast_to(lanes[:, None, :], (2, 8, HALF)).copy()
-    return first, second, octet, rows.copy(), between, coarse, lanes
+    return first, second, octet, rows.copy(), between, shift, coarse, lanes
 
 
 def lane_butterfly(real, imag, lanes_real, lanes_imag):
@@ -69,43 +71,113 @@
     )
 
 
-def make_kernel(slots):
-    def kernel(
-        plan_ref, edge_ref, strain_ref, wave_ref, first_ref, second_ref, octet_ref, rows_ref, between_ref,
-        coarse_ref, lanes_ref, out_ref, q_ref, p_ref, x_ref, o_ref, l_ref, z_ref, fold_ref, peak_ref,
-    ):
-        step = pl.program_id(0)
-
-        @pl.when(step == 0)
-        def _():
-            out_ref[...] = jnp.zeros_like(out_ref)
-
-        @pl.when(step < plan_ref[slots])
-        def _():
+def encode_kernel(core_ref, strain_ref, real_ref, imag_ref):
+    rows = strain_ref.shape[2]
+    for which in range(2):
+        segment = core_ref[0] if which == 0 else 1 - core_ref[0]
+        data = [strain_ref[segment, 0], strain_ref[segment, 1]]
+        largest = jnp.max(jnp.maximum(jnp.abs(data[0]), jnp.abs(data[1])), axis=1, keepdims=True)
+        exponent = jnp.floor(jnp.log2(jnp.maximum(largest, 1e-30)) + 1.001)
+        scale = jnp.exp2(15.0 - exponent)
+        for value, out_ref in zip(data, (real_ref, imag_ref)):
+            number = jnp.clip(jnp.round(value * scale), -32767.0, 32767.0).astype(jnp.int32)
+            packed = (number[:, :HALF] << 16) | (number[:, HALF:] & 0xFFFF)
+            out_ref[which, 0:rows, :] = packed[:, :128]
+            out_ref[which, rows : 2 * rows, :] = packed[:, 128:]
+        spread = jnp.broadcast_to(exponent.astype(jnp.int32), (rows, 128))
+        same = lax.broadcasted_iota(jnp.int32, (rows, 128), 0) == lax.broadcasted_iota(jnp.int32, (rows, 128), 1)
+        line = jnp.sum(jnp.where(same, spread, 0), axis=0, keepdims=True)
+        real_ref[which, 2 * rows :, :] = jnp.broadcast_to(line, (8, 128))
+
+
+def encode(core, strain):
+    rows = strain.shape[2]
+    return pl.pallas_call(
+        encode_kernel,
+        out_shape=(
+            jax.ShapeDtypeStruct((2, 2 * rows + 8, 128), jnp.int32),
+            jax.ShapeDtypeStruct((2, 2 * rows, 128), jnp.int32),
+        ),
+        in_specs=[pl.BlockSpec(memory_space=pltpu.SMEM), pl.BlockSpec(memory_space=pltpu.VMEM)],
+        out_specs=(pl.BlockSpec(memory_space=pltpu.VMEM), pl.BlockSpec(memory_space=pltpu.VMEM)),
+    )(core.reshape(1), strain)
+
+
+def make_kernel(slots, real_masks, imag_masks):
+    blocks = [len(masks) for masks in (real_masks, imag_masks)]
+
+    def kernel(*refs):
+        plan_ref, edge_ref, own_ref, mate_ref = refs[:4]
+        real_refs = refs[4 : 4 + blocks[0]]
+        imag_refs = refs[4 + blocks[0] : 4 + sum(blocks)]
+        (first_ref, second_ref, octet_ref, rows_ref, base_ref, shift_ref, coarse_ref, lanes_ref, out_ref, strain_ref,
+         wave_ref, between_ref, q_ref, p_ref, x_ref, o_ref, l_ref, z_ref, fold_ref, peak_ref, sem) = refs[4 + sum(blocks) :]
+        live = plan_ref[slots]
+        own_count = plan_ref[slots + 1]
+        device = plan_ref[slots + 2]
+
+        def fetch(step):
             slot = plan_ref[step]
-            core = plan_ref[slots + 1]
+            buffer = step % 2
+
+            @pl.when(step < own_count)
+            def _():
+                pltpu.make_async_copy(own_ref.at[slot], wave_ref.at[buffer], sem.at[buffer]).start()
+
+            @pl.when(step >= own_count)
+            def _():
+                pltpu.make_async_copy(mate_ref.at[slot - slots // 2], wave_ref.at[buffer], sem.at[buffer]).start()
+
+        fetch(0)
+        out_ref[...] = jnp.zeros_like(out_ref)
+
+        held = imag_refs[0].shape[1] // 2
+        same = lax.broadcasted_iota(jnp.int32, (held, 128), 0) == lax.broadcasted_iota(jnp.int32, (held, 128), 1)
+        for part, (part_refs, masks) in enumerate(((real_refs, real_masks), (imag_refs, imag_masks))):
+            for ref, group in zip(part_refs, masks):
+                for i, mask in enumerate(group):
+                    row = pl.multiple_of((device ^ mask) * held, held)
+                    if part == 0:
+                        line = jnp.broadcast_to(ref[i, 2 * held : 2 * held + 1, :], (held, 128))
+                        exponent = jnp.sum(jnp.where(same, line, 0).astype(jnp.float32), axis=1, keepdims=True)
+                        scale = jnp.broadcast_to(jnp.exp2(exponent - 15.0), (held, 128))
+                        strain_ref[2, pl.ds(row, held), 0:128] = scale
+                    scale = strain_ref[2, pl.ds(row, held), 0:128]
+                    for tile in range(2):
+                        word = ref[i, tile * held : (tile + 1) * held, :]
+                        high = (word >> 16).astype(jnp.float32) * scale
+                        low = ((word << 16) >> 16).astype(jnp.float32) * scale
+                        strain_ref[part, pl.ds(row, held), tile * 128 : tile * 128 + 128] = high
+                        strain_ref[part, pl.ds(row, held), HALF + tile * 128 : HALF + tile * 128 + 128] = low
+
+        for v in range(4):
+            for mirror in range(2):
+                at = mirror * 4 + v
+                base_r = base_ref[0]
+                base_i = base_ref[1] if mirror == 0 else -base_ref[1]
+                shift_r = shift_ref[0, at : at + 1, :]
+                shift_i = shift_ref[1, at : at + 1, :]
+                between_ref[v, mirror, 0] = base_r * shift_r - base_i * shift_i
+                between_ref[v, mirror, 1] = base_r * shift_i + base_i * shift_r
+
+        def one_slot(step, carry):
+            slot = plan_ref[step]
+            buffer = step % 2
             base = slot * (BINS + 1)
             first_edge = edge_ref[base]
             last_edge = edge_ref[base + BINS]
 
-            held = strain_ref.shape[3]
-            piece = min(held, 16)
-
-            def strain_rows(part, r):
-                pieces = []
-                for i in range(16 // piece):
-                    row = r + i * piece
-                    owner = row // held
-                    which = (owner + core) % 2
-                    inner = pl.multiple_of(row % held, piece)
-                    pieces.append(strain_ref[owner // 2, which, part, pl.ds(inner, piece), :])
-                return pieces[0] if len(pieces) == 1 else jnp.concatenate(pieces, axis=0)
+            @pl.when(step + 1 < live)
+            def _():
+                fetch(step + 1)
+
+            pltpu.make_async_copy(own_ref.at[0], wave_ref.at[buffer], sem.at[buffer]).wait()
 
             def product(r):
-                data_r = strain_rows(0, r)
-                data_i = strain_rows(1, r)
-                wave_r = wave_ref[0, 0, pl.ds(r, 16), :].astype(jnp.float32)
-                wave_i = wave_ref[0, 1, pl.ds(r, 16), :].astype(jnp.float32)
+                data_r = strain_ref[0, pl.ds(r, 16), :]
+                data_i = strain_ref[1, pl.ds(r, 16), :]
+                wave_r = wave_ref[buffer, 0, pl.ds(r, 16), :].astype(jnp.float32)
+                wave_i = wave_ref[buffer, 1, pl.ds(r, 16), :].astype(jnp.float32)
                 index = (
                     lax.broadcasted_iota(jnp.int32, (16, ROWS), 0) * ROWS
                     + lax.broadcasted_iota(jnp.int32, (16, ROWS), 1)
@@ -132,10 +204,13 @@
                 for v in range(4):
                     real, imag = mixed[v]
                     if v != 2:
-                        at = (0, 1, 0, 2)[v]
+                        at = (1, 0, 0, 0)[v]
                         cosine = jnp.concatenate([rows_ref[at, 0, pl.ds(r, 16), :]] * 4, axis=1)
                         sine = jnp.concatenate([rows_ref[at, 1, pl.ds(r, 16), :]] * 4, axis=1)
-                        real, imag = real * cosine - imag * sine, real * sine + imag * cosine
+                        if v == 3:
+                            real, imag = real * cosine - imag * sine, real * sine + imag * cosine
+                        else:
+                            real, imag = real * cosine + imag * sine, imag * cosine - real * sine
                     for part, value in ((0, real), (1, imag)):
                         high, low = split_bf16(value)
                         column = (2 * v + part) * ROWS
@@ -283,77 +358,88 @@
                     top = jnp.maximum(top, jnp.sqrt(loud[:, lane : lane + 128]) * factor)
             best = jnp.max(top, axis=(0, 1), keepdims=True) / jnp.sqrt(energy)
             out_ref[pl.ds(slot, 1), :] = jnp.broadcast_to(best, (1, 128))
+            return carry
+
+        lax.fori_loop(0, live, one_slot, 0)
 
     return kernel
 
 
-def slot_peaks(plan, edges, strain, waves, interpret=False):
-    slots = waves.shape[0]
+def slot_peaks(plan, edges, own_waves, mate_waves, real_blocks, imag_blocks, real_masks, imag_masks):
+    slots = 2 * own_waves.shape[0]
     tables = [jnp.asarray(table) for table in host_tables()]
-
-    def resident(array):
-        return pl.BlockSpec(
-            array.shape, lambda i, plan, edges, n=array.ndim: (0,) * n, pipeline_mode=pl.Buffered(1)
-        )
-
+    smem = pl.BlockSpec(memory_space=pltpu.SMEM)
+    hbm = pl.BlockSpec(memory_space=pl.ANY)
+    vmem = pl.BlockSpec(memory_space=pltpu.VMEM)
     return pl.pallas_call(
-        make_kernel(slots),
+        make_kernel(slots, real_masks, imag_masks),
         out_shape=jax.ShapeDtypeStruct((slots, 128), jnp.float32),
-        grid_spec=pltpu.PrefetchScalarGridSpec(
-            num_scalar_prefetch=2,
-            grid=(slots,),
-            in_specs=[
-                resident(strain),
-                pl.BlockSpec((1, 2, ROWS, ROWS), lambda i, plan, edges: (plan[i], 0, 0, 0)),
-            ]
-            + [resident(table) for table in tables],
-            out_specs=pl.BlockSpec((slots, 128), lambda i, plan, edges: (0, 0)),
-            scratch_shapes=[
-                pltpu.VMEM((2, ROWS, ROWS), jnp.float32),
-                pltpu.VMEM((ROWS, ROWS), jnp.float32),
-                pltpu.VMEM((ROWS, 8 * ROWS), jnp.bfloat16),
-                pltpu.VMEM((HALF, 2 * ROWS), jnp.float32),
-                pltpu.VMEM((1024, ROWS), jnp.bfloat16),
-                pltpu.VMEM((1024, HALF), jnp.float32),
-                pltpu.VMEM((16, BINS * ROWS), jnp.float32),
-                pltpu.VMEM((8, 8, ROWS), jnp.float32),
-            ],
-        ),
+        in_specs=[smem, smem, hbm, hbm] + [vmem] * (len(real_blocks) + len(imag_blocks) + len(tables)),
+        out_specs=vmem,
+        scratch_shapes=[
+            pltpu.VMEM((3, ROWS, ROWS), jnp.float32),
+            pltpu.VMEM((2, 2, ROWS, ROWS), jnp.bfloat16),
+            pltpu.VMEM((4, 2, 2, QUART, ROWS), jnp.float32),
+            pltpu.VMEM((2, ROWS, ROWS), jnp.float32),
+            pltpu.VMEM((ROWS, ROWS), jnp.float32),
+            pltpu.VMEM((ROWS, 8 * ROWS), jnp.bfloat16),
+            pltpu.VMEM((HALF, 2 * ROWS), jnp.float32),
+            pltpu.VMEM((1024, ROWS), jnp.bfloat16),
+            pltpu.VMEM((1024, HALF), jnp.float32),
+            pltpu.VMEM((16, BINS * ROWS), jnp.float32),
+            pltpu.VMEM((8, 8, ROWS), jnp.float32),
+            pltpu.SemaphoreType.DMA((2,)),
+        ],
         compiler_params=pltpu.CompilerParams(vmem_limit_bytes=48 << 20),
-        interpret=interpret,
-    )(plan, edges, strain, waves, *tables)
+    )(plan, edges, own_waves, mate_waves, *real_blocks, *imag_blocks, *tables)
+
+
+def exchange(x, bit):
+    devices = lax.axis_size("bank")
+    return lax.ppermute(x, "bank", [(i, i ^ bit) for i in range(devices)])
 
 
 def per_device(strain, templates, counts, edges):
     devices = lax.axis_size("bank")
-    device = lax.axis_index("bank")
+    device = lax.axis_index("bank").astype(jnp.int32)
     core = device % 2
     slots = templates.shape[0]
-    mates = [(i, i ^ 1) for i in range(devices)]
-    cores = [list(range(c, devices, 2)) for c in range(2)]
-
-    shard = strain.reshape(2, 2, -1, ROWS)
-    own = lax.dynamic_index_in_dim(shard, core, 0, keepdims=False)
-    other = lax.dynamic_index_in_dim(shard, 1 - core, 0, keepdims=False)
-    shard = jnp.stack([own, lax.ppermute(other, "bank", mates)])
-    spectrum = lax.all_gather(shard, "bank", axis=0, tiled=False, axis_index_groups=cores)
+    bits = [1 << i for i in range(1, devices.bit_length() - 1)]
+    orders = [bits[::-1], bits[:1] + bits[:0:-1]]
+
+    coded = encode(core, strain.reshape(2, 2, -1, ROWS))
+    current = [jnp.stack([part[0], exchange(part[1], 1)]) for part in coded]
+    masks = [[0, 1], [0, 1]]
+    for level in range(len(bits)):
+        arrived = [exchange(current[half], orders[half][level]) for half in range(2)]
+        added = [[m ^ orders[half][level] for m in masks[half]] for half in range(2)]
+        if level + 1 < len(bits):
+            current = [jnp.concatenate([current[half], arrived[half]]) for half in range(2)]
+            masks = [masks[half] + added[half] for half in range(2)]
+    blocks = [[current[half], arrived[half]] for half in range(2)]
+    block_masks = [[masks[half], added[half]] for half in range(2)]
 
     small = jnp.concatenate([counts, edges.reshape(-1)])
-    mate_small = lax.ppermute(small, "bank", mates)
-    mate_waves = lax.ppermute(templates, "bank", mates)
-    waves = jnp.concatenate([templates, mate_waves]).reshape(2 * slots, 2, ROWS, ROWS)
+    mate_small = exchange(small, 1)
+    own_waves = templates.reshape(slots, 2, ROWS, ROWS)
+    mate_waves = exchange(own_waves, 1)
     own_count = small[0]
     live = own_count + mate_small[0]
     ramp = jnp.minimum(jnp.arange(2 * slots, dtype=jnp.int32), live - 1)
     order = jnp.where(ramp < own_count, ramp, slots + ramp - own_count)
-    plan = jnp.concatenate([order, live[None], core[None]]).astype(jnp.int32)
+    plan = jnp.concatenate([order, live[None], own_count[None], device[None]]).astype(jnp.int32)
     all_edges = jnp.concatenate([small[1:], mate_small[1:]])
-    peaks = slot_peaks(plan, all_edges, spectrum, waves)[:, 0]
+    peaks = slot_peaks(plan, all_edges, own_waves, mate_waves, *blocks, *block_masks)[:, 0]
 
     mine = peaks[:slots]
-    theirs = lax.ppermute(peaks[slots:], "bank", mates)
+    here = jnp.max(peaks)
+    theirs = exchange(jnp.concatenate([peaks[slots:], here[None]]), 1)
+    there = theirs[slots]
+    theirs = theirs[:slots]
     slot_peak = jnp.where(core == 0, jnp.stack([mine, theirs], axis=1), jnp.stack([theirs, mine], axis=1))
-    segment_peak = lax.pmax(jnp.max(slot_peak, axis=0), "bank")
+    segment_peak = jnp.where(core == 0, jnp.stack([here, there]), jnp.stack([there, here]))
+    for bit in bits:
+        segment_peak = jnp.maximum(segment_peak, exchange(segment_peak, bit))
     return (slot_peak, segment_peak)
 
 

time: 160 us -> 109 us (0.68)
  blocking collectives: 30.2 us -> 0 us
  starting transfers between devices: 1.19 us -> 22.7 us
  between operations: 14.9 us -> 1.55 us
  Pallas kernels: 50.8 us -> 40.2 us
  other arithmetic: 14.3 us -> 6.27 us
  local copies, waits for them, and re-layouts: 16.8 us -> 11.2 us
  waiting for transfers between devices: 31.1 us -> 26.6 us
    pmax x1 -> x0, blocking collectives: 30.2 us -> none  [per_device(): segment_peak = lax.pmax(jnp.max(slot_peak, axis=0), 'bank')]
    all_gather x1 -> x0, waiting for transfers between devices: 26.4 us -> none  [per_device(): lax.all_gather(shard, 'bank', axis=0, tiled=False, axis_index_groups=cores)]
    ppermute x4 -> x14, waiting for transfers between devices: 4.61 us -> 26.6 us  [exchange(): return lax.ppermute(x, 'bank', [(i, i ^ bit) for i in range(devices)])]
    ppermute x4 -> x14, starting transfers between devices: 1.16 us -> 22.7 us  [exchange(): return lax.ppermute(x, 'bank', [(i, i ^ bit) for i in range(devices)])]
    concatenate x2 -> x6, other arithmetic: 13.3 us -> 0.86 us  [the longest x1 0.72 us: per_device(): theirs = exchange(jnp.concatenate([peaks[slots:], here[None]]), 1)]
    pallas_call x1 -> x2, Pallas kernels: 50.8 us -> 40.2 us  [the longest x1 38.5 us: slot_peaks(): pl.pallas_call(make_kernel(slots, real_masks, imag_masks), out_shape=jax....]
    reshape x2, local copies, waits for them, and re-layouts: 13.5 us -> 7.89 us  [the longest x1 6.95 us: per_device(): own_waves = templates.reshape(slots, 2, ROWS, ROWS)]
    max x0 -> x3, other arithmetic: none -> 3.21 us  [per_device(): segment_peak = jnp.maximum(segment_peak, exchange(segment_peak, bit))]
  transfers between devices with their start and end apart: 5 -> 14, of which waited for: 3 -> 11; matrix products, arithmetic and copies ran while one was open for 18% -> 3% of each run, Pallas kernels for 0% -> 2%
where the time goes in v2:
time: 109 us; the launch traced here: 108 us
  Pallas kernels  40.2 us (37%)
  waiting for transfers between devices  26.6 us (24%)
  starting transfers between devices  22.7 us (21%)
  local copies, waits for them, and re-layouts  11.2 us (10%)
  other arithmetic  6.27 us (6%)
  between operations  1.55 us (1%)
    pallas_call x1, Pallas kernels, slot_peaks(): pl.pallas_call(make_kernel(slots, real_masks, imag_masks), out_shape=jax....  38.5 us
    ppermute x14, waiting for transfers between devices, exchange(): return lax.ppermute(x, 'bank', [(i, i ^ bit) for i in range(devices)])  26.6 us
    ppermute x14, starting transfers between devices, exchange(): return lax.ppermute(x, 'bank', [(i, i ^ bit) for i in range(devices)])  22.7 us
    reshape x1, local copies, waits for them, and re-layouts, per_device(): own_waves = templates.reshape(slots, 2, ROWS, ROWS)  6.95 us
    max x3, other arithmetic, per_device(): segment_peak = jnp.maximum(segment_peak, exchange(segment_peak, bit))  3.21 us
  transfers between devices with their start and end apart: 14, of which 11 were waited for; matrix products, arithmetic and copies ran while one was open for 3% of the time, Pallas kernels for 2%

profile of v2, /device:TPU:0, one launch (start us, length us, event | category | flops | bytes accessed | tf_op | source)
XLA Modules:
  0.0 108.4 jit_solution(15783409868372843656)
XLA Ops:
  0.8 7.0 %reshape.20.refs_2_ = bf16[4,2,512,512]{3,2,1,0:T(8,128)(2,1)} reshape(bf16[4,2,262144]{2,1,0:T(2,128)(2,1)} %param.13) | data formatting | bytes 8388608 | tf_op jit(solution)/shard_map/reshape | solution.py:424
  7.7 0.5 collective-permute-start.1
  8.2 0.9 reshape.22.strain_ref
  9.1 1.7 %shard_map.131 = (s32[2,72,128]{2,1,0:T(8,128)}, s32[2,64,128]{2,1,0:T(8,128)}) custom-call(s32[1]{0:T(128)} %bitcast.4.core_ref, f32[2,2,32,512]{3,2,1,0:T(8,128)} %reshape.22.strain_ref), custom_call_target="tpu_custom_call" | custom-call | tf_op jit(solution)/shard_map/pallas_call | solution.py:95
  10.8 0.8 fusion.1
  11.7 0.8 fusion
  12.5 0.5 collective-permute-start.2
  13.7 1.3 %collective-permute-done.6 = s32[64,128]{1,0:T(8,128)S(1)} collective-permute-done((s32[64,128]{1,0:T(8,128)S(1)}, s32[64,128]{1,0:T(8,128)S(1)}, u32[]{:S(2)}, u32[]{:S(2)}) %collective-permute-start.6) | collective-permute-done | bytes 32800 | tf_op jit(solution)/shard_map/ppermute | solution.py:399
  15.0 2.9 %collective-permute-start.7 = (s32[2,64,128]{2,1,0:T(8,128)S(1)}, s32[2,64,128]{2,1,0:T(8,128)S(1)}, u32[]{:S(2)}, u32[]{:S(2)}) collective-permute-start(s32[2,64,128]{2,1,0:T(8,128)S(1)} %pad_add_fusion.5), channel_id=1, source_target_pairs={{0,2},{1,3},{2,0},{3,1},{4,6},{5,7},{6,4},{7,5},{8,10},{9,11},{10,... | collective-permute-start | bytes 196616 | tf_op jit(solution)/shard_map/ppermute | solution.py:399
  17.9 2.7 %collective-permute-start.3 = (s32[2,72,128]{2,1,0:T(8,128)S(1)}, s32[2,72,128]{2,1,0:T(8,128)S(1)}, u32[]{:S(2)}, u32[]{:S(2)}) collective-permute-start(s32[2,72,128]{2,1,0:T(8,128)S(1)} %pad_add_fusion.4), channel_id=1, source_target_pairs={{0,8},{1,9},{2,10},{3,11},{4,12},{5,13},{6,14},{7,15},{8,0},{9,1},... | collective-permute-start | bytes 221192 | tf_op jit(solution)/shard_map/ppermute | solution.py:399
  20.5 2.8 %collective-permute-start.8 = (s32[4,64,128]{2,1,0:T(8,128)S(1)}, s32[4,64,128]{2,1,0:T(8,128)S(1)}, u32[]{:S(2)}, u32[]{:S(2)}) collective-permute-start(s32[4,64,128]{2,1,0:T(8,128)S(1)} %pad_add_fusion.3), channel_id=1, source_target_pairs={{0,8},{1,9},{2,10},{3,11},{4,12},{5,13},{6,14},{7,15},{8,0},{9,1},... | collective-permute-start | bytes 393224 | tf_op jit(solution)/shard_map/ppermute | solution.py:399
  23.3 4.7 %collective-permute-done.3 = s32[2,72,128]{2,1,0:T(8,128)S(1)} collective-permute-done((s32[2,72,128]{2,1,0:T(8,128)S(1)}, s32[2,72,128]{2,1,0:T(8,128)S(1)}, u32[]{:S(2)}, u32[]{:S(2)}) %collective-permute-start.3) | collective-permute-done | bytes 73760 | tf_op jit(solution)/shard_map/ppermute | solution.py:399
  28.4 1.1 %collective-permute-done = s32[69]{0:T(128)S(1)} collective-permute-done((s32[69]{0:T(128)S(1)}, s32[69]{0:T(128)S(1)}, u32[]{:S(2)}, u32[]{:S(2)}) %collective-permute-start) | collective-permute-done | bytes 308 | tf_op jit(solution)/shard_map/ppermute | solution.py:399
  29.6 0.8 collective-permute-done.8
  30.4 1.1 collective-permute-start.9
  31.5 2.4 %collective-permute-done.4 = s32[4,72,128]{2,1,0:T(8,128)S(1)} collective-permute-done((s32[4,72,128]{2,1,0:T(8,128)S(1)}, s32[4,72,128]{2,1,0:T(8,128)S(1)}, u32[]{:S(2)}, u32[]{:S(2)}) %collective-permute-start.4) | collective-permute-done | bytes 147488 | tf_op jit(solution)/shard_map/ppermute | solution.py:399
  34.2 4.7 %collective-permute-done.9.refs_7_ = s32[8,64,128]{2,1,0:T(8,128)S(1)} collective-permute-done((s32[8,64,128]{2,1,0:T(8,128)S(1)}, s32[8,64,128]{2,1,0:T(8,128)S(1)}, u32[]{:S(2)}, u32[]{:S(2)}) %collective-permute-start.9) | collective-permute-done | bytes 262176 | tf_op jit(solution)/shard_map/ppermute | solution.py:399
  38.9 1.8 %collective-permute-done.5.refs_5_ = s32[8,72,128]{2,1,0:T(8,128)S(1)} collective-permute-done((s32[8,72,128]{2,1,0:T(8,128)S(1)}, s32[8,72,128]{2,1,0:T(8,128)S(1)}, u32[]{:S(2)}, u32[]{:S(2)}) %collective-permute-start.5) | collective-permute-done | bytes 294944 | tf_op jit(solution)/shard_map/ppermute | solution.py:399
  40.8 38.5 %shard_map.132 = f32[8,128]{1,0:T(8,128)S(1)} custom-call(s32[11]{0:T(128)S(1)} %pad_add_fusion.8.refs_0_, s32[136]{0:T(256)S(1)} %pad_add_fusion.6.refs_1_, bf16[4,2,512,512]{3,2,1,0:T(8,128)(2,1)} %reshape.20.refs_2_, bf16[4,2,512,512]{3,2,1,0:T(8,128)(2,1)} %collective-permute-done.1.refs_3_, s32[8,72,128]{2,1,0:T(8,128)S(1)} %pad_add_fusion.refs_4_, ...), custom_call_target="tpu_custom_call" | custom-call | tf_op jit(solution)/shard_map/pallas_call | solution.py:374
  79.2 0.6 slice_reduce_fusion
  80.0 0.7 pad_maximum_fusion
  80.7 1.1 %collective-permute-done.10 = f32[5]{0:T(128)S(1)} collective-permute-done((f32[5]{0:T(128)S(1)}, f32[5]{0:T(128)S(1)}, u32[]{:S(2)}, u32[]{:S(2)}) %collective-permute-start.10) | collective-permute-done | bytes 52 | tf_op jit(solution)/shard_map/ppermute | solution.py:399
  81.9 0.6 slice.50
  82.5 1.3 %broadcast_select_fusion = f32[2]{0:T(128)S(1)} fusion(pred[]{:T(512)S(6)} %eq.6, f32[1]{0:T(128)} %slice.50, f32[1]{0:T(128)} %bitcast.9), kind=kLoop, calls=%fused_computation.13 | loop fusion | flops 6 | bytes 17 | tf_op jit(solution)/shard_map/jit(_where)/select_n | solution.py:440
  83.9 0.7 copy.19
  84.6 3.5 %collective-permute-done.11 = f32[2]{0:T(128)S(1)} collective-permute-done((f32[2]{0:T(128)S(1)}, f32[2]{0:T(128)S(1)}, u32[]{:S(2)}, u32[]{:S(2)}) %collective-permute-start.11) | collective-permute-done | bytes 40 | tf_op jit(solution)/shard_map/ppermute | solution.py:399
  88.1 1.3 %fusion.3 = f32[2]{0:T(128)S(1)} fusion(f32[2]{0:T(128)S(1)} %collective-permute-done.11, f32[1]{0:T(128)} %bitcast.9, f32[1]{0:T(128)} %slice.50, pred[]{:T(512)S(6)} %eq.6), kind=kLoop, calls=%fused_computation.21 | loop fusion | flops 8 | bytes 25 | tf_op jit(solution)/shard_map/max | solution.py:442
  89.5 3.5 %collective-permute-done.12 = f32[2]{0:T(128)S(1)} collective-permute-done((f32[2]{0:T(128)S(1)}, f32[2]{0:T(128)S(1)}, u32[]{:S(2)}, u32[]{:S(2)}) %collective-permute-start.12) | collective-permute-done | bytes 40 | tf_op jit(solution)/shard_map/ppermute | solution.py:399
  93.0 1.3 %fusion.4 = f32[2]{0:T(128)S(1)} fusion(f32[2]{0:T(128)S(1)} %collective-permute-done.12, f32[2]{0:T(128)S(1)} %collective-permute-done.11, f32[1]{0:T(128)} %bitcast.9, f32[1]{0:T(128)} %slice.50, pred[]{:T(512)S(6)} %eq.6), kind=kLoop, calls=%fused_computation.22 | loop fusion | flops 10 | bytes 33 | tf_op jit(solution)/shard_map/max | solution.py:442
  94.4 12.0 %collective-permute-start.13 = (f32[2]{0:T(128)S(1)}, f32[2]{0:T(128)S(1)}, u32[]{:S(2)}, u32[]{:S(2)}) collective-permute-start(f32[2]{0:T(128)S(1)} %fusion.4), channel_id=1, source_target_pairs={{0,8},{1,9},{2,10},{3,11},{4,12},{5,13},{6,14},{7,15},{8,0},{9,1},... | collective-permute-start | bytes 32 | tf_op jit(solution)/shard_map/ppermute | solution.py:399
  106.4 1.5 %collective-permute-done.13 = f32[2]{0:T(128)S(1)} collective-permute-done((f32[2]{0:T(128)S(1)}, f32[2]{0:T(128)S(1)}, u32[]{:S(2)}, u32[]{:S(2)}) %collective-permute-start.13) | collective-permute-done | bytes 40 | tf_op jit(solution)/shard_map/ppermute | solution.py:399
  107.9 0.5 max.11
  (46 shorter events, 1.2 us)
Async XLA Ops:
  0.6 40.1 %copy-start = (f32[2,128,512]{2,1,0:T(8,128)S(1)}, f32[2,128,512]{2,1,0:T(8,128)}, u32[]{:S(2)}) copy-start(f32[2,128,512]{2,1,0:T(8,128)} %constant.45.clone.refs_12_) | copy-start | bytes 1572868
  0.6 40.1 %copy-start.1 = (f32[2,2,256,128]{3,2,1,0:T(8,128)S(1)}, f32[2,2,256,128]{3,2,1,0:T(8,128)}, u32[]{:S(2)}) copy-start(f32[2,2,256,128]{3,2,1,0:T(8,128)} %constant.44.clone.refs_11_) | copy-start | bytes 1572868
  0.7 40.0 %copy-start.2 = (bf16[768,256]{1,0:T(8,128)(2,1)S(1)}, bf16[768,256]{1,0:T(8,128)(2,1)}, u32[]{:S(2)}) copy-start(bf16[768,256]{1,0:T(8,128)(2,1)} %constant.42.clone.refs_9_) | copy-start | bytes 1179652
  0.7 40.0 %copy-start.3 = (bf16[256,768]{1,0:T(8,128)(2,1)S(1)}, bf16[256,768]{1,0:T(8,128)(2,1)}, u32[]{:S(2)}) copy-start(bf16[256,768]{1,0:T(8,128)(2,1)} %constant.41.clone.refs_8_) | copy-start | bytes 1179652
  0.7 40.0 %copy-start.4 = (f32[2,8,512]{2,1,0:T(8,128)S(1)}, f32[2,8,512]{2,1,0:T(8,128)}, u32[]{:S(2)}) copy-start(f32[2,8,512]{2,1,0:T(8,128)} %constant.47.clone.refs_14_) | copy-start | bytes 98308
  0.7 40.0 %copy-start.5 = (f32[2,8,512]{2,1,0:T(8,128)S(1)}, f32[2,8,512]{2,1,0:T(8,128)}, u32[]{:S(2)}) copy-start(f32[2,8,512]{2,1,0:T(8,128)} %constant.46.clone.refs_13_) | copy-start | bytes 98308
  0.7 40.0 %copy-start.6 = (f32[2,8,256]{2,1,0:T(8,128)S(1)}, f32[2,8,256]{2,1,0:T(8,128)}, u32[]{:S(2)}) copy-start(f32[2,8,256]{2,1,0:T(8,128)} %constant.48.clone.refs_15_) | copy-start | bytes 49156
  0.7 40.0 %copy-start.7 = (bf16[16,48]{1,0:T(8,128)(2,1)S(1)}, bf16[16,48]{1,0:T(8,128)(2,1)}, u32[]{:S(2)}) copy-start(bf16[16,48]{1,0:T(8,128)(2,1)} %constant.43.clone.refs_10_) | copy-start | bytes 4612
  0.7 7.4 %copy-start.8 = (f32[2,2,16384]{2,1,0:T(2,128)S(1)}, f32[2,2,16384]{2,1,0:T(2,128)}, u32[]{:S(2)}) copy-start(f32[2,2,16384]{2,1,0:T(2,128)} %param.12) | copy-start | bytes 786436
  0.7 12.8 %copy-start.9 = (s32[4,17]{1,0:T(4,128)S(1)}, s32[4,17]{1,0:T(4,128)}, u32[]{:S(2)}) copy-start(s32[4,17]{1,0:T(4,128)} %param.15) | copy-start | bytes 820
  7.7 33.0 %collective-permute-start.1 = (bf16[4,2,512,512]{3,2,1,0:T(8,128)(2,1)}, bf16[4,2,512,512]{3,2,1,0:T(8,128)(2,1)}, u32[]{:S(2)}, u32[]{:S(2)}) collective-permute-start(bf16[4,2,512,512]{3,2,1,0:T(8,128)(2,1)} %reshape.20.refs_2_), channel_id=1, source_target_pairs={{0,1},{1,0},{2,3},{3,2},{4,5},{5,4},{6,7},{7,6},{8,9},{9,8},{10,11... | collective-permute-start | bytes 12582920 | tf_op jit(solution)/shard_map/ppermute | solution.py:399
  11.6 3.4 %collective-permute-start.6 = (s32[64,128]{1,0:T(8,128)S(1)}, s32[64,128]{1,0:T(8,128)S(1)}, u32[]{:S(2)}, u32[]{:S(2)}) collective-permute-start(s32[64,128]{1,0:T(8,128)S(1)} %get-tuple-element.13), channel_id=1, source_target_pairs={{0,1},{1,0},{2,3},{3,2},{4,5},{5,4},{6,7},{7,6},{8,9},{9,8},{10,11... | collective-permute-start | bytes 98312 | tf_op jit(solution)/shard_map/ppermute | solution.py:399
  12.5 5.4 %collective-permute-start.2 = (s32[72,128]{1,0:T(8,128)S(1)}, s32[72,128]{1,0:T(8,128)S(1)}, u32[]{:S(2)}, u32[]{:S(2)}) collective-permute-start(s32[72,128]{1,0:T(8,128)S(1)} %get-tuple-element.11), channel_id=1, source_target_pairs={{0,1},{1,0},{2,3},{3,2},{4,5},{5,4},{6,7},{7,6},{8,9},{9,8},{10,11... | collective-permute-start | bytes 110600 | tf_op jit(solution)/shard_map/ppermute | solution.py:399
  15.0 5.5 %collective-permute-start.7 = (s32[2,64,128]{2,1,0:T(8,128)S(1)}, s32[2,64,128]{2,1,0:T(8,128)S(1)}, u32[]{:S(2)}, u32[]{:S(2)}) collective-permute-start(s32[2,64,128]{2,1,0:T(8,128)S(1)} %pad_add_fusion.5), channel_id=1, source_target_pairs={{0,2},{1,3},{2,0},{3,1},{4,6},{5,7},{6,4},{7,5},{8,10},{9,11},{10,... | collective-permute-start | bytes 196616 | tf_op jit(solution)/shard_map/ppermute | solution.py:399
  17.9 10.2 %collective-permute-start.3 = (s32[2,72,128]{2,1,0:T(8,128)S(1)}, s32[2,72,128]{2,1,0:T(8,128)S(1)}, u32[]{:S(2)}, u32[]{:S(2)}) collective-permute-start(s32[2,72,128]{2,1,0:T(8,128)S(1)} %pad_add_fusion.4), channel_id=1, source_target_pairs={{0,8},{1,9},{2,10},{3,11},{4,12},{5,13},{6,14},{7,15},{8,0},{9,1},... | collective-permute-start | bytes 221192 | tf_op jit(solution)/shard_map/ppermute | solution.py:399
  20.5 9.8 %collective-permute-start.8 = (s32[4,64,128]{2,1,0:T(8,128)S(1)}, s32[4,64,128]{2,1,0:T(8,128)S(1)}, u32[]{:S(2)}, u32[]{:S(2)}) collective-permute-start(s32[4,64,128]{2,1,0:T(8,128)S(1)} %pad_add_fusion.3), channel_id=1, source_target_pairs={{0,8},{1,9},{2,10},{3,11},{4,12},{5,13},{6,14},{7,15},{8,0},{9,1},... | collective-permute-start | bytes 393224 | tf_op jit(solution)/shard_map/ppermute | solution.py:399
  28.1 5.8 %collective-permute-start.4 = (s32[4,72,128]{2,1,0:T(8,128)S(1)}, s32[4,72,128]{2,1,0:T(8,128)S(1)}, u32[]{:S(2)}, u32[]{:S(2)}) collective-permute-start(s32[4,72,128]{2,1,0:T(8,128)S(1)} %pad_add_fusion.2), channel_id=1, source_target_pairs={{0,4},{1,5},{2,6},{3,7},{4,0},{5,1},{6,2},{7,3},{8,12},{9,13},{10,... | collective-permute-start | bytes 442376 | tf_op jit(solution)/shard_map/ppermute | solution.py:399
  28.4 1.1 %collective-permute-start = (s32[69]{0:T(128)S(1)}, s32[69]{0:T(128)S(1)}, u32[]{:S(2)}, u32[]{:S(2)}) collective-permute-start(s32[69]{0:T(128)S(1)} %pad_add_fusion.7), channel_id=1, source_target_pairs={{0,1},{1,0},{2,3},{3,2},{4,5},{5,4},{6,7},{7,6},{8,9},{9,8},{10,11... | collective-permute-start | bytes 836 | tf_op jit(solution)/shard_map/ppermute | solution.py:399
  30.4 8.5 %collective-permute-start.9 = (s32[8,64,128]{2,1,0:T(8,128)S(1)}, s32[8,64,128]{2,1,0:T(8,128)S(1)}, u32[]{:S(2)}, u32[]{:S(2)}) collective-permute-start(s32[8,64,128]{2,1,0:T(8,128)S(1)} %pad_add_fusion.1.refs_6_), channel_id=1, source_target_pairs={{0,4},{1,5},{2,6},{3,7},{4,0},{5,1},{6,2},{7,3},{8,12},{9,13},{10,... | collective-permute-start | bytes 786440 | tf_op jit(solution)/shard_map/ppermute | solution.py:399
  33.9 6.8 %collective-permute-start.5 = (s32[8,72,128]{2,1,0:T(8,128)S(1)}, s32[8,72,128]{2,1,0:T(8,128)S(1)}, u32[]{:S(2)}, u32[]{:S(2)}) collective-permute-start(s32[8,72,128]{2,1,0:T(8,128)S(1)} %pad_add_fusion.refs_4_), channel_id=1, source_target_pairs={{0,2},{1,3},{2,0},{3,1},{4,6},{5,7},{6,4},{7,5},{8,10},{9,11},{10,... | collective-permute-start | bytes 884744 | tf_op jit(solution)/shard_map/ppermute | solution.py:399
  80.7 1.1 %collective-permute-start.10 = (f32[5]{0:T(128)S(1)}, f32[5]{0:T(128)S(1)}, u32[]{:S(2)}, u32[]{:S(2)}) collective-permute-start(f32[5]{0:T(128)S(1)} %pad_maximum_fusion), channel_id=1, source_target_pairs={{0,1},{1,0},{2,3},{3,2},{4,5},{5,4},{6,7},{7,6},{8,9},{9,8},{10,11... | collective-permute-start | bytes 68 | tf_op jit(solution)/shard_map/ppermute | solution.py:399
  84.6 3.5 %collective-permute-start.11 = (f32[2]{0:T(128)S(1)}, f32[2]{0:T(128)S(1)}, u32[]{:S(2)}, u32[]{:S(2)}) collective-permute-start(f32[2]{0:T(128)S(1)} %broadcast_select_fusion), channel_id=1, source_target_pairs={{0,2},{1,3},{2,0},{3,1},{4,6},{5,7},{6,4},{7,5},{8,10},{9,11},{10,... | collective-permute-start | bytes 32 | tf_op jit(solution)/shard_map/ppermute | solution.py:399
  89.5 3.5 %collective-permute-start.12 = (f32[2]{0:T(128)S(1)}, f32[2]{0:T(128)S(1)}, u32[]{:S(2)}, u32[]{:S(2)}) collective-permute-start(f32[2]{0:T(128)S(1)} %fusion.3), channel_id=1, source_target_pairs={{0,4},{1,5},{2,6},{3,7},{4,0},{5,1},{6,2},{7,3},{8,12},{9,13},{10,... | collective-permute-start | bytes 32 | tf_op jit(solution)/shard_map/ppermute | solution.py:399
  94.4 13.5 %collective-permute-start.13 = (f32[2]{0:T(128)S(1)}, f32[2]{0:T(128)S(1)}, u32[]{:S(2)}, u32[]{:S(2)}) collective-permute-start(f32[2]{0:T(128)S(1)} %fusion.4), channel_id=1, source_target_pairs={{0,8},{1,9},{2,10},{3,11},{4,12},{5,13},{6,14},{7,15},{8,0},{9,1},... | collective-permute-start | bytes 32 | tf_op jit(solution)/shard_map/ppermute | solution.py:399

commit v3 on v2

--- a/solution.py
+++ b/solution.py
@@ -409,6 +409,7 @@
 
     coded = encode(core, strain.reshape(2, 2, -1, ROWS))
     current = [jnp.stack([part[0], exchange(part[1], 1)]) for part in coded]
+    templates, *current = lax.optimization_barrier((templates, *current))
     masks = [[0, 1], [0, 1]]
     for level in range(len(bits)):
         arrived = [exchange(current[half], orders[half][level]) for half in range(2)]
@@ -429,18 +430,16 @@
     order = jnp.where(ramp < own_count, ramp, slots + ramp - own_count)
     plan = jnp.concatenate([order, live[None], own_count[None], device[None]]).astype(jnp.int32)
     all_edges = jnp.concatenate([small[1:], mate_small[1:]])
-    peaks = slot_peaks(plan, all_edges, own_waves, mate_waves, *blocks, *block_masks)[:, 0]
-
-    mine = peaks[:slots]
-    here = jnp.max(peaks)
-    theirs = exchange(jnp.concatenate([peaks[slots:], here[None]]), 1)
-    there = theirs[slots]
-    theirs = theirs[:slots]
-    slot_peak = jnp.where(core == 0, jnp.stack([mine, theirs], axis=1), jnp.stack([theirs, mine], axis=1))
-    segment_peak = jnp.where(core == 0, jnp.stack([here, there]), jnp.stack([there, here]))
+    peaks = slot_peaks(plan, all_edges, own_waves, mate_waves, *blocks, *block_masks)
+
+    mine = lax.broadcasted_iota(jnp.int32, peaks.shape, 1) % 2 == core
+    arrived = exchange(peaks, 1)
+    swapped = jnp.concatenate([arrived[slots:], arrived[:slots]])
+    both = jnp.where(mine, peaks, swapped)
+    best = both
     for bit in bits:
-        segment_peak = jnp.maximum(segment_peak, exchange(segment_peak, bit))
-    return (slot_peak, segment_peak)
+        best = jnp.maximum(best, exchange(best, bit))
+    return (both[:slots, :2], jnp.max(best, axis=0)[:2])
 
 
 def solution(mesh):

time: 109 us -> 109 us (level)
  starting transfers between devices: 22.7 us -> 44.5 us
  Pallas kernels: 40.2 us -> 22 us
  other arithmetic: 6.27 us -> 0.82 us
  waiting for transfers between devices: 26.6 us -> 29 us
    ppermute x14, starting transfers between devices: 22.7 us -> 44.5 us  [exchange(): return lax.ppermute(x, 'bank', [(i, i ^ bit) for i in range(devices)])]
    pallas_call x1, Pallas kernels: 38.5 us -> 20.2 us  [slot_peaks(): pl.pallas_call(make_kernel(slots, real_masks, imag_masks), out_shape=jax....]
    max x3 -> x2, other arithmetic: 3.21 us -> 0.01 us  [per_device(): best = jnp.maximum(best, exchange(best, bit))]
    ppermute x14, waiting for transfers between devices: 26.6 us -> 29 us  [exchange(): return lax.ppermute(x, 'bank', [(i, i ^ bit) for i in range(devices)])]
    select_n x2 -> x1, other arithmetic: 1.42 us -> 0.01 us  [per_device(): both = jnp.where(mine, peaks, swapped)]
  transfers between devices with their start and end apart: 14 -> 14, of which waited for: 11 -> 11; matrix products, arithmetic and copies ran while one was open for 3% -> 2% of each run, Pallas kernels for 2% -> 0%
where the time goes in v3:
time: 109 us
  starting transfers between devices  44.5 us (41%)
  waiting for transfers between devices  29 us (27%)
  Pallas kernels  22 us (20%)
  local copies, waits for them, and re-layouts  11.3 us (10%)
  between operations  1.55 us (1%)
    ppermute x14, starting transfers between devices, exchange(): return lax.ppermute(x, 'bank', [(i, i ^ bit) for i in range(devices)])  44.5 us
    ppermute x14, waiting for transfers between devices, exchange(): return lax.ppermute(x, 'bank', [(i, i ^ bit) for i in range(devices)])  29 us
    pallas_call x1, Pallas kernels, slot_peaks(): pl.pallas_call(make_kernel(slots, real_masks, imag_masks), out_shape=jax....  20.2 us
    reshape x1, local copies, waits for them, and re-layouts, per_device(): own_waves = templates.reshape(slots, 2, ROWS, ROWS)  6.94 us
  transfers between devices with their start and end apart: 14, of which 11 were waited for; matrix products, arithmetic and copies ran while one was open for 2% of the time, Pallas kernels for 0%

profile of v3, /device:TPU:0, one launch (start us, length us, event | category | flops | bytes accessed | tf_op | source)
XLA Modules:
  0.0 109.1 jit_solution(11986357456118443264)
XLA Ops:
  0.6 1.9 %reshape.18.strain_ref = f32[2,2,32,512]{3,2,1,0:T(8,128)} reshape(f32[2,2,16384]{2,1,0:T(2,128)} %param.12) | data formatting | bytes 524288 | tf_op jit(solution)/shard_map/reshape | solution.py:410
  2.5 1.7 %shard_map.131 = (s32[2,72,128]{2,1,0:T(8,128)}, s32[2,64,128]{2,1,0:T(8,128)}) custom-call(s32[1]{0:T(128)} %bitcast.4.core_ref, f32[2,2,32,512]{3,2,1,0:T(8,128)} %reshape.18.strain_ref), custom_call_target="tpu_custom_call" | custom-call | tf_op jit(solution)/shard_map/pallas_call | solution.py:95
  4.2 0.8 fusion.1
  5.0 0.5 collective-permute-start.2
  5.5 0.8 fusion
  6.3 1.1 %collective-permute-done.1 = s32[72,128]{1,0:T(8,128)S(1)} collective-permute-done((s32[72,128]{1,0:T(8,128)S(1)}, s32[72,128]{1,0:T(8,128)S(1)}, u32[]{:S(2)}, u32[]{:S(2)}) %collective-permute-start.1) | collective-permute-done | bytes 36896 | tf_op jit(solution)/shard_map/ppermute | solution.py:399
  7.6 6.9 %reshape.19.refs_2_ = bf16[4,2,512,512]{3,2,1,0:T(8,128)(2,1)} reshape(bf16[4,2,262144]{2,1,0:T(2,128)(2,1)} %param.13) | data formatting | bytes 8388608 | tf_op jit(solution)/shard_map/reshape | solution.py:425
  14.5 0.2 collective-permute-start.3
  15.3 0.1 reshape.16
  15.4 0.1 pad_add_fusion.5
  15.5 0.4 collective-permute-start
  15.9 5.8 %collective-permute-done = s32[69]{0:T(128)S(1)} collective-permute-done((s32[69]{0:T(128)S(1)}, s32[69]{0:T(128)S(1)}, u32[]{:S(2)}, u32[]{:S(2)}) %collective-permute-start) | collective-permute-done | bytes 308 | tf_op jit(solution)/shard_map/ppermute | solution.py:399
  21.7 2.7 %collective-permute-start.7 = (s32[2,64,128]{2,1,0:T(8,128)S(1)}, s32[2,64,128]{2,1,0:T(8,128)S(1)}, u32[]{:S(2)}, u32[]{:S(2)}) collective-permute-start(s32[2,64,128]{2,1,0:T(8,128)S(1)} %pad_add_fusion.3), channel_id=1, source_target_pairs={{0,2},{1,3},{2,0},{3,1},{4,6},{5,7},{6,4},{7,5},{8,10},{9,11},{10,... | collective-permute-start | bytes 196616 | tf_op jit(solution)/shard_map/ppermute | solution.py:399
  24.4 2.6 %collective-permute-start.4 = (s32[2,72,128]{2,1,0:T(8,128)S(1)}, s32[2,72,128]{2,1,0:T(8,128)S(1)}, u32[]{:S(2)}, u32[]{:S(2)}) collective-permute-start(s32[2,72,128]{2,1,0:T(8,128)S(1)} %pad_add_fusion.2), channel_id=1, source_target_pairs={{0,8},{1,9},{2,10},{3,11},{4,12},{5,13},{6,14},{7,15},{8,0},{9,1},... | collective-permute-start | bytes 221192 | tf_op jit(solution)/shard_map/ppermute | solution.py:399
  27.0 2.9 %collective-permute-start.8 = (s32[4,64,128]{2,1,0:T(8,128)S(1)}, s32[4,64,128]{2,1,0:T(8,128)S(1)}, u32[]{:S(2)}, u32[]{:S(2)}) collective-permute-start(s32[4,64,128]{2,1,0:T(8,128)S(1)} %pad_add_fusion.1), channel_id=1, source_target_pairs={{0,8},{1,9},{2,10},{3,11},{4,12},{5,13},{6,14},{7,15},{8,0},{9,1},... | collective-permute-start | bytes 393224 | tf_op jit(solution)/shard_map/ppermute | solution.py:399
  29.9 4.7 %collective-permute-done.4 = s32[2,72,128]{2,1,0:T(8,128)S(1)} collective-permute-done((s32[2,72,128]{2,1,0:T(8,128)S(1)}, s32[2,72,128]{2,1,0:T(8,128)S(1)}, u32[]{:S(2)}, u32[]{:S(2)}) %collective-permute-start.4) | collective-permute-done | bytes 73760 | tf_op jit(solution)/shard_map/ppermute | solution.py:399
  34.6 0.2 collective-permute-start.5
  34.8 2.2 %collective-permute-done.8 = s32[4,64,128]{2,1,0:T(8,128)S(1)} collective-permute-done((s32[4,64,128]{2,1,0:T(8,128)S(1)}, s32[4,64,128]{2,1,0:T(8,128)S(1)}, u32[]{:S(2)}, u32[]{:S(2)}) %collective-permute-start.8) | collective-permute-done | bytes 131104 | tf_op jit(solution)/shard_map/ppermute | solution.py:399
  37.0 0.5 collective-permute-start.9
  37.5 3.5 %collective-permute-done.5 = s32[4,72,128]{2,1,0:T(8,128)S(1)} collective-permute-done((s32[4,72,128]{2,1,0:T(8,128)S(1)}, s32[4,72,128]{2,1,0:T(8,128)S(1)}, u32[]{:S(2)}, u32[]{:S(2)}) %collective-permute-start.5) | collective-permute-done | bytes 147488 | tf_op jit(solution)/shard_map/ppermute | solution.py:399
  41.3 4.3 %collective-permute-done.9.refs_7_ = s32[8,64,128]{2,1,0:T(8,128)S(1)} collective-permute-done((s32[8,64,128]{2,1,0:T(8,128)S(1)}, s32[8,64,128]{2,1,0:T(8,128)S(1)}, u32[]{:S(2)}, u32[]{:S(2)}) %collective-permute-start.9) | collective-permute-done | bytes 262176 | tf_op jit(solution)/shard_map/ppermute | solution.py:399
  45.6 2.2 %collective-permute-done.6.refs_5_ = s32[8,72,128]{2,1,0:T(8,128)S(1)} collective-permute-done((s32[8,72,128]{2,1,0:T(8,128)S(1)}, s32[8,72,128]{2,1,0:T(8,128)S(1)}, u32[]{:S(2)}, u32[]{:S(2)}) %collective-permute-start.6) | collective-permute-done | bytes 294944 | tf_op jit(solution)/shard_map/ppermute | solution.py:399
  47.9 20.2 %shard_map.132 = f32[8,128]{1,0:T(8,128)S(1)} custom-call(s32[11]{0:T(128)S(1)} %pad_add_fusion.6.refs_0_, s32[136]{0:T(256)S(1)} %pad_add_fusion.4.refs_1_, bf16[4,2,512,512]{3,2,1,0:T(8,128)(2,1)} %reshape.19.refs_2_, bf16[4,2,512,512]{3,2,1,0:T(8,128)(2,1)} %collective-permute-done.3.refs_3_, s32[8,72,128]{2,1,0:T(8,128)S(1)} %constant_dynamic-update-slice_fusion.refs_4_, ...), custom_call_target="tpu_custom_call" | custom-call | tf_op jit(solution)/shard_map/pallas_call | solution.py:374
  68.2 1.1 %collective-permute-done.10 = f32[8,128]{1,0:T(8,128)S(1)} collective-permute-done((f32[8,128]{1,0:T(8,128)S(1)}, f32[8,128]{1,0:T(8,128)S(1)}, u32[]{:S(2)}, u32[]{:S(2)}) %collective-permute-start.10) | collective-permute-done | bytes 4128 | tf_op jit(solution)/shard_map/ppermute | solution.py:399
  69.3 9.5 %collective-permute-start.11 = (f32[8,128]{1,0:T(8,128)S(1)}, f32[8,128]{1,0:T(8,128)S(1)}, u32[]{:S(2)}, u32[]{:S(2)}) collective-permute-start(f32[8,128]{1,0:T(8,128)S(1)} %maximum_select_fusion), channel_id=1, source_target_pairs={{0,2},{1,3},{2,0},{3,1},{4,6},{5,7},{6,4},{7,5},{8,10},{9,11},{10,... | collective-permute-start | bytes 12296 | tf_op jit(solution)/shard_map/ppermute | solution.py:399
  78.8 1.6 %collective-permute-done.11 = f32[8,128]{1,0:T(8,128)S(1)} collective-permute-done((f32[8,128]{1,0:T(8,128)S(1)}, f32[8,128]{1,0:T(8,128)S(1)}, u32[]{:S(2)}, u32[]{:S(2)}) %collective-permute-start.11) | collective-permute-done | bytes 4128 | tf_op jit(solution)/shard_map/ppermute | solution.py:399
  80.4 11.4 %collective-permute-start.12 = (f32[8,128]{1,0:T(8,128)S(1)}, f32[8,128]{1,0:T(8,128)S(1)}, u32[]{:S(2)}, u32[]{:S(2)}) collective-permute-start(f32[8,128]{1,0:T(8,128)S(1)} %max.9), channel_id=1, source_target_pairs={{0,4},{1,5},{2,6},{3,7},{4,0},{5,1},{6,2},{7,3},{8,12},{9,13},{10,... | collective-permute-start | bytes 12296 | tf_op jit(solution)/shard_map/ppermute | solution.py:399
  91.8 1.6 %collective-permute-done.12 = f32[8,128]{1,0:T(8,128)S(1)} collective-permute-done((f32[8,128]{1,0:T(8,128)S(1)}, f32[8,128]{1,0:T(8,128)S(1)}, u32[]{:S(2)}, u32[]{:S(2)}) %collective-permute-start.12) | collective-permute-done | bytes 4128 | tf_op jit(solution)/shard_map/ppermute | solution.py:399
  93.3 13.6 %collective-permute-start.13 = (f32[8,128]{1,0:T(8,128)S(1)}, f32[8,128]{1,0:T(8,128)S(1)}, u32[]{:S(2)}, u32[]{:S(2)}) collective-permute-start(f32[8,128]{1,0:T(8,128)S(1)} %max.10), channel_id=1, source_target_pairs={{0,8},{1,9},{2,10},{3,11},{4,12},{5,13},{6,14},{7,15},{8,0},{9,1},... | collective-permute-start | bytes 12296 | tf_op jit(solution)/shard_map/ppermute | solution.py:399
  107.0 0.7 copy.14
  107.6 0.9 collective-permute-done.13
  108.6 0.5 maximum_reduce_fusion
  (45 shorter events, 0.6 us)
Async XLA Ops:
  5.0 1.3 %collective-permute-start.2 = (s32[64,128]{1,0:T(8,128)S(1)}, s32[64,128]{1,0:T(8,128)S(1)}, u32[]{:S(2)}, u32[]{:S(2)}) collective-permute-start(s32[64,128]{1,0:T(8,128)S(1)} %get-tuple-element.17), channel_id=1, source_target_pairs={{0,1},{1,0},{2,3},{3,2},{4,5},{5,4},{6,7},{7,6},{8,9},{9,8},{10,11... | collective-permute-start | bytes 98312 | tf_op jit(solution)/shard_map/ppermute | solution.py:399
  6.3 1.2 %collective-permute-start.1 = (s32[72,128]{1,0:T(8,128)S(1)}, s32[72,128]{1,0:T(8,128)S(1)}, u32[]{:S(2)}, u32[]{:S(2)}) collective-permute-start(s32[72,128]{1,0:T(8,128)S(1)} %get-tuple-element.15), channel_id=1, source_target_pairs={{0,1},{1,0},{2,3},{3,2},{4,5},{5,4},{6,7},{7,6},{8,9},{9,8},{10,11... | collective-permute-start | bytes 110600 | tf_op jit(solution)/shard_map/ppermute | solution.py:399
  7.5 7.9 %copy-start.8 = (s32[4,17]{1,0:T(4,128)S(1)}, s32[4,17]{1,0:T(4,128)}, u32[]{:S(2)}) copy-start(s32[4,17]{1,0:T(4,128)} %param.15) | copy-start | bytes 820
  7.5 40.3 %copy-start = (f32[2,128,512]{2,1,0:T(8,128)S(1)}, f32[2,128,512]{2,1,0:T(8,128)}, u32[]{:S(2)}) copy-start(f32[2,128,512]{2,1,0:T(8,128)} %constant.53.clone.refs_12_) | copy-start | bytes 1572868
  7.5 40.3 %copy-start.1 = (f32[2,2,256,128]{3,2,1,0:T(8,128)S(1)}, f32[2,2,256,128]{3,2,1,0:T(8,128)}, u32[]{:S(2)}) copy-start(f32[2,2,256,128]{3,2,1,0:T(8,128)} %constant.52.clone.refs_11_) | copy-start | bytes 1572868
  7.5 40.3 %copy-start.2 = (bf16[768,256]{1,0:T(8,128)(2,1)S(1)}, bf16[768,256]{1,0:T(8,128)(2,1)}, u32[]{:S(2)}) copy-start(bf16[768,256]{1,0:T(8,128)(2,1)} %constant.50.clone.refs_9_) | copy-start | bytes 1179652
  7.5 40.3 %copy-start.3 = (bf16[256,768]{1,0:T(8,128)(2,1)S(1)}, bf16[256,768]{1,0:T(8,128)(2,1)}, u32[]{:S(2)}) copy-start(bf16[256,768]{1,0:T(8,128)(2,1)} %constant.49.clone.refs_8_) | copy-start | bytes 1179652
  7.5 40.3 %copy-start.4 = (f32[2,8,512]{2,1,0:T(8,128)S(1)}, f32[2,8,512]{2,1,0:T(8,128)}, u32[]{:S(2)}) copy-start(f32[2,8,512]{2,1,0:T(8,128)} %constant.55.clone.refs_14_) | copy-start | bytes 98308
  7.5 40.3 %copy-start.5 = (f32[2,8,512]{2,1,0:T(8,128)S(1)}, f32[2,8,512]{2,1,0:T(8,128)}, u32[]{:S(2)}) copy-start(f32[2,8,512]{2,1,0:T(8,128)} %constant.54.clone.refs_13_) | copy-start | bytes 98308
  7.6 40.3 %copy-start.6 = (f32[2,8,256]{2,1,0:T(8,128)S(1)}, f32[2,8,256]{2,1,0:T(8,128)}, u32[]{:S(2)}) copy-start(f32[2,8,256]{2,1,0:T(8,128)} %constant.56.clone.refs_15_) | copy-start | bytes 49156
  7.6 40.3 %copy-start.7 = (bf16[16,48]{1,0:T(8,128)(2,1)S(1)}, bf16[16,48]{1,0:T(8,128)(2,1)}, u32[]{:S(2)}) copy-start(bf16[16,48]{1,0:T(8,128)(2,1)} %constant.51.clone.refs_10_) | copy-start | bytes 4612
  14.5 33.3 %collective-permute-start.3 = (bf16[4,2,512,512]{3,2,1,0:T(8,128)(2,1)}, bf16[4,2,512,512]{3,2,1,0:T(8,128)(2,1)}, u32[]{:S(2)}, u32[]{:S(2)}) collective-permute-start(bf16[4,2,512,512]{3,2,1,0:T(8,128)(2,1)} %reshape.19.refs_2_), channel_id=1, source_target_pairs={{0,1},{1,0},{2,3},{3,2},{4,5},{5,4},{6,7},{7,6},{8,9},{9,8},{10,11... | collective-permute-start | bytes 12582920 | tf_op jit(solution)/shard_map/ppermute | solution.py:399
  15.5 6.1 %collective-permute-start = (s32[69]{0:T(128)S(1)}, s32[69]{0:T(128)S(1)}, u32[]{:S(2)}, u32[]{:S(2)}) collective-permute-start(s32[69]{0:T(128)S(1)} %pad_add_fusion.5), channel_id=1, source_target_pairs={{0,1},{1,0},{2,3},{3,2},{4,5},{5,4},{6,7},{7,6},{8,9},{9,8},{10,11... | collective-permute-start | bytes 836 | tf_op jit(solution)/shard_map/ppermute | solution.py:399
  21.7 5.3 %collective-permute-start.7 = (s32[2,64,128]{2,1,0:T(8,128)S(1)}, s32[2,64,128]{2,1,0:T(8,128)S(1)}, u32[]{:S(2)}, u32[]{:S(2)}) collective-permute-start(s32[2,64,128]{2,1,0:T(8,128)S(1)} %pad_add_fusion.3), channel_id=1, source_target_pairs={{0,2},{1,3},{2,0},{3,1},{4,6},{5,7},{6,4},{7,5},{8,10},{9,11},{10,... | collective-permute-start | bytes 196616 | tf_op jit(solution)/shard_map/ppermute | solution.py:399
  24.4 10.2 %collective-permute-start.4 = (s32[2,72,128]{2,1,0:T(8,128)S(1)}, s32[2,72,128]{2,1,0:T(8,128)S(1)}, u32[]{:S(2)}, u32[]{:S(2)}) collective-permute-start(s32[2,72,128]{2,1,0:T(8,128)S(1)} %pad_add_fusion.2), channel_id=1, source_target_pairs={{0,8},{1,9},{2,10},{3,11},{4,12},{5,13},{6,14},{7,15},{8,0},{9,1},... | collective-permute-start | bytes 221192 | tf_op jit(solution)/shard_map/ppermute | solution.py:399
  27.0 9.9 %collective-permute-start.8 = (s32[4,64,128]{2,1,0:T(8,128)S(1)}, s32[4,64,128]{2,1,0:T(8,128)S(1)}, u32[]{:S(2)}, u32[]{:S(2)}) collective-permute-start(s32[4,64,128]{2,1,0:T(8,128)S(1)} %pad_add_fusion.1), channel_id=1, source_target_pairs={{0,8},{1,9},{2,10},{3,11},{4,12},{5,13},{6,14},{7,15},{8,0},{9,1},... | collective-permute-start | bytes 393224 | tf_op jit(solution)/shard_map/ppermute | solution.py:399
  34.6 6.4 %collective-permute-start.5 = (s32[4,72,128]{2,1,0:T(8,128)S(1)}, s32[4,72,128]{2,1,0:T(8,128)S(1)}, u32[]{:S(2)}, u32[]{:S(2)}) collective-permute-start(s32[4,72,128]{2,1,0:T(8,128)S(1)} %pad_add_fusion), channel_id=1, source_target_pairs={{0,4},{1,5},{2,6},{3,7},{4,0},{5,1},{6,2},{7,3},{8,12},{9,13},{10,... | collective-permute-start | bytes 442376 | tf_op jit(solution)/shard_map/ppermute | solution.py:399
  37.0 8.7 %collective-permute-start.9 = (s32[8,64,128]{2,1,0:T(8,128)S(1)}, s32[8,64,128]{2,1,0:T(8,128)S(1)}, u32[]{:S(2)}, u32[]{:S(2)}) collective-permute-start(s32[8,64,128]{2,1,0:T(8,128)S(1)} %constant_dynamic-update-slice_fusion.3.refs_6_), channel_id=1, source_target_pairs={{0,4},{1,5},{2,6},{3,7},{4,0},{5,1},{6,2},{7,3},{8,12},{9,13},{10,... | collective-permute-start | bytes 786440 | tf_op jit(solution)/shard_map/ppermute | solution.py:399
  41.0 6.8 %collective-permute-start.6 = (s32[8,72,128]{2,1,0:T(8,128)S(1)}, s32[8,72,128]{2,1,0:T(8,128)S(1)}, u32[]{:S(2)}, u32[]{:S(2)}) collective-permute-start(s32[8,72,128]{2,1,0:T(8,128)S(1)} %constant_dynamic-update-slice_fusion.refs_4_), channel_id=1, source_target_pairs={{0,2},{1,3},{2,0},{3,1},{4,6},{5,7},{6,4},{7,5},{8,10},{9,11},{10,... | collective-permute-start | bytes 884744 | tf_op jit(solution)/shard_map/ppermute | solution.py:399
  68.1 1.2 %collective-permute-start.10 = (f32[8,128]{1,0:T(8,128)S(1)}, f32[8,128]{1,0:T(8,128)S(1)}, u32[]{:S(2)}, u32[]{:S(2)}) collective-permute-start(f32[8,128]{1,0:T(8,128)S(1)} %shard_map.132), channel_id=1, source_target_pairs={{0,1},{1,0},{2,3},{3,2},{4,5},{5,4},{6,7},{7,6},{8,9},{9,8},{10,11... | collective-permute-start | bytes 12296 | tf_op jit(solution)/shard_map/ppermute | solution.py:399
  69.3 11.0 %collective-permute-start.11 = (f32[8,128]{1,0:T(8,128)S(1)}, f32[8,128]{1,0:T(8,128)S(1)}, u32[]{:S(2)}, u32[]{:S(2)}) collective-permute-start(f32[8,128]{1,0:T(8,128)S(1)} %maximum_select_fusion), channel_id=1, source_target_pairs={{0,2},{1,3},{2,0},{3,1},{4,6},{5,7},{6,4},{7,5},{8,10},{9,11},{10,... | collective-permute-start | bytes 12296 | tf_op jit(solution)/shard_map/ppermute | solution.py:399
  80.4 12.9 %collective-permute-start.12 = (f32[8,128]{1,0:T(8,128)S(1)}, f32[8,128]{1,0:T(8,128)S(1)}, u32[]{:S(2)}, u32[]{:S(2)}) collective-permute-start(f32[8,128]{1,0:T(8,128)S(1)} %max.9), channel_id=1, source_target_pairs={{0,4},{1,5},{2,6},{3,7},{4,0},{5,1},{6,2},{7,3},{8,12},{9,13},{10,... | collective-permute-start | bytes 12296 | tf_op jit(solution)/shard_map/ppermute | solution.py:399
  93.3 15.2 %collective-permute-start.13 = (f32[8,128]{1,0:T(8,128)S(1)}, f32[8,128]{1,0:T(8,128)S(1)}, u32[]{:S(2)}, u32[]{:S(2)}) collective-permute-start(f32[8,128]{1,0:T(8,128)S(1)} %max.10), channel_id=1, source_target_pairs={{0,8},{1,9},{2,10},{3,11},{4,12},{5,13},{6,14},{7,15},{8,0},{9,1},... | collective-permute-start | bytes 12296 | tf_op jit(solution)/shard_map/ppermute | solution.py:399
